TPU v7x, 128 devices: a whole 4x4x4 slice. The times are simulated.
128 devices in a mesh: dp: 16 (over z, y_hi, core), tensor: 8 (over x, y_lo).
Axes of the slice: x: 4, y: 4 (y_hi: 2, y_lo: 2; y = y_hi * 2 + y_lo), z: 4, core: 2. Of those that a mesh axis runs over, the one named last changes fastest.
Arguments:
- history: bfloat16 [4, 3072, 4096], P(None, 'dp'), may hold values from -6 to 6
- depth_weights: float32 [4], replicated, may hold values from 0.2 to 1
- depth_index: int32 [4], replicated, may hold values from 0 to 3
- gain: float32 [4096], replicated, may hold values from 0.1 to 1.9
- gate_blocks: bfloat16 [896, 128, 128], P(('tensor', 'dp')), may hold values from -0.1875 to 0.1875
- up_blocks: bfloat16 [896, 128, 128], P(('tensor', 'dp')), may hold values from -0.1875 to 0.1875
- down_blocks: bfloat16 [896, 128, 128], P(('tensor', 'dp')), may hold values from -0.09375 to 0.09375
- block_ids: int32 [896, 2], P('tensor'), may hold values from 0 to 31, as said below
- grad_out: bfloat16 [3072, 4096], P('dp'), may hold values from -16 to 16
Outputs:
- layer_out: bfloat16 [3072, 4096], P('dp', 'tensor')
- grad_mixed: float32 [3072, 4096], P('dp', 'tensor')
- grad_gate: float32 [896, 128, 128], P(('tensor', 'dp'))
- grad_up: float32 [896, 128, 128], P(('tensor', 'dp'))
- grad_down: float32 [896, 128, 128], P(('tensor', 'dp'))
- grad_depth: float32 [4], replicated
- grad_gain: float32 [4096], P('tensor')
Inputs may be any that keep to these rules, and one draw needn't show every extreme that they name: `block_ids`: within the 112 rows of one index of tensor the pairs are distinct; column 0 is a row block below 32, column 1 a column block below 14 counted within that index's hidden units.
All inputs are finite; a program needn't handle non-finite values.
Results may differ from a plain program's by a relative error of at most 0.025.
Values may be sent and summed in bfloat16 or wider, within the bound.
No kernel may reach another device: no remote copies, remote signals or barrier semaphores. Data moves between devices by JAX's collectives and lax.ppermute only.
A program may use at most 192 MiB of HBM per device.

v0:
```python
import functools

import jax
import jax.numpy as jnp
from jax import lax
from jax.experimental import pallas as pl
from jax.experimental.pallas import tpu as pltpu
from jax.sharding import PartitionSpec as P


EPSILON = 1e-05
BS = 128
N_Z, N_Y, N_CORE = 4, 2, 2
N_X, N_YLO = 4, 2
N_DP = N_Z * N_Y * N_CORE
N_TENSOR = N_X * N_YLO
CHIPS = N_Z * N_Y
OWN, YY, A1, B1, A2, YA, YB, Y2 = range(8)
AHEAD = (0, 0, -1, 1, 2, -1, 1, 2)
TURN = (0, 1, 0, 0, 0, 1, 1, 1)
EARLY = [(chip, flip) for chip in (OWN, A1, B1, YY) for flip in range(2)]
LATE = [(chip, flip) for chip in (A2, YA, YB, Y2) for flip in range(2)]
FIRST = (Y2, YB, YA, A1)
SECOND = (A2, B1, YY, OWN)
FIRST_SLOTS = [(chip, flip) for chip in FIRST for flip in range(2)]
SECOND_SLOTS = [(chip, flip) for chip in SECOND for flip in range(2)]
TABLE = EARLY + LATE + FIRST_SLOTS + SECOND_SLOTS
AT_EARLY, AT_LATE, AT_FIRST, AT_SECOND = 0, 8, 16, 24
EXTRA = 16
TILE = 16
ROWS = 32
VMEM_LIMIT = 60 * 1024 * 1024


BF = jnp.bfloat16
F32 = jnp.float32


def sign_of(core):
    return 1 - 2 * core


def dp_perm(kind):
    pairs = []
    for z in range(N_Z):
        for y in range(N_Y):
            for core in range(N_CORE):
                tz, ty, tc = z, y, core
                if kind == "a":
                    tz = (z + sign_of(core)) % N_Z
                elif kind == "b":
                    tz = (z - sign_of(core)) % N_Z
                elif kind == "y":
                    ty = 1 - y
                elif kind == "c":
                    tc = 1 - core
                elif kind == "z1":
                    tz = z ^ 1
                elif kind == "z2":
                    tz = z ^ 2
                elif kind == "z3":
                    tz = z ^ 3
                elif kind == "yc":
                    ty, tc = 1 - y, 1 - core
                pairs.append(((z * N_Y + y) * N_CORE + core, (tz * N_Y + ty) * N_CORE + tc))
    return pairs


def tensor_perm(kind):
    pairs = []
    for dp in range(N_DP):
        step = sign_of(dp % N_CORE)
        for x in range(N_X):
            for ylo in range(N_YLO):
                tx, ty = x, ylo
                if kind == "a":
                    tx = (x + step) % N_X
                elif kind == "b":
                    tx = (x - step) % N_X
                elif kind == "y":
                    ty = 1 - ylo
                else:
                    tx = x ^ int(kind)
                pairs.append((dp * N_TENSOR + x * N_YLO + ylo, dp * N_TENSOR + tx * N_YLO + ty))
    return pairs


def over_dp(value, kind):
    return lax.ppermute(value, "dp", dp_perm(kind))


def over_tensor(value, kind):
    return lax.ppermute(value, ("dp", "tensor"), tensor_perm(kind))


def spec(space):
    return pl.BlockSpec(memory_space=space)


def lanes(index, size=BS):
    return pl.ds(pl.multiple_of(index * size, size), size)


def mm(left, right):
    return jnp.dot(left, right, preferred_element_type=F32)


def mm_t(left, right):
    return lax.dot_general(left, right, (((1,), (1,)), ((), ())), preferred_element_type=F32)


def mm_l(left, right):
    return lax.dot_general(left, right, (((0,), (0,)), ((), ())), preferred_element_type=F32)


def fold(value):
    return sum(value[:, k * BS : (k + 1) * BS] for k in range(value.shape[1] // BS))


def norm_kernel(index, weights, h0, h1, h2, h3, grad_out, gain, normed, stats, kept):
    tile, width = normed.shape
    size = 512
    zero = jnp.zeros((tile, BS), F32)
    squares, moments, cots = zero, [zero] * 4, [zero] * 4
    for at in range(0, width, size):
        cut = slice(at, at + size)
        layers = [h[0, :, cut].astype(F32) for h in (h0, h1, h2, h3)]
        mixed = weights[0] * layers[0]
        for slot in range(1, 4):
            mixed = mixed + weights[slot] * layers[slot]
        kept[:, cut] = mixed
        squares = squares + fold(mixed * mixed)
        cot = grad_out[:, cut].astype(F32)
        for slot in range(4):
            moments[slot] = moments[slot] + fold(mixed * layers[slot])
            cots[slot] = cots[slot] + fold(cot * layers[slot])
    scale = lax.rsqrt(jnp.sum(squares, axis=-1, keepdims=True) / width + EPSILON)
    for at in range(0, width, size):
        cut = slice(at, at + size)
        normed[:, cut] = (kept[:, cut] * scale * gain[:, cut]).astype(BF)
    lane = lax.broadcasted_iota(jnp.int32, stats.shape, 1)
    found = jnp.where(lane == 0, scale, 0.0)
    for slot in range(4):
        found = jnp.where(lane == 1 + slot, jnp.sum(moments[slot], axis=-1, keepdims=True), found)
        found = jnp.where(lane == 5 + slot, jnp.sum(cots[slot], axis=-1, keepdims=True), found)
    stats[...] = found


def norm_call(depth_index, depth_weights, history, grad_out, gain):
    tokens, width = grad_out.shape

    def layer_spec(slot):
        return pl.BlockSpec((1, TILE, width), lambda i, index: (index[slot], i, 0))

    return pl.pallas_call(
        norm_kernel,
        out_shape=(
            jax.ShapeDtypeStruct((tokens, width), BF),
            jax.ShapeDtypeStruct((tokens, BS), F32),
            jax.ShapeDtypeStruct((tokens, width), F32),
        ),
        grid_spec=pltpu.PrefetchScalarGridSpec(
            num_scalar_prefetch=1,
            grid=(tokens // TILE,),
            in_specs=[spec(pltpu.SMEM)]
            + [layer_spec(slot) for slot in range(4)]
            + [
                pl.BlockSpec((TILE, width), lambda i, index: (i, 0)),
                pl.BlockSpec((1, width), lambda i, index: (0, 0)),
            ],
            out_specs=[
                pl.BlockSpec((TILE, width), lambda i, index: (i, 0)),
                pl.BlockSpec((TILE, BS), lambda i, index: (i, 0)),
                pl.BlockSpec((TILE, width), lambda i, index: (i, 0)),
            ],
        ),
        compiler_params=pltpu.CompilerParams(vmem_limit_bytes=VMEM_LIMIT),
        cost_estimate=pl.CostEstimate(flops=tokens * width * 30, bytes_accessed=tokens * width * 12, transcendentals=0),
        name="norm",
    )(depth_index, depth_weights, history, history, history, history, grad_out, gain.reshape(1, width))


def join_kernel(gate, up, down, out, sems):
    share = gate.shape[0]
    copies = [
        pltpu.make_async_copy(ref, out.at[pl.ds(k * share, share)], sems.at[k])
        for k, ref in enumerate((gate, up, down))
    ]
    for copy in copies:
        copy.start()
    for copy in copies:
        copy.wait()


def join_call(gate, up, down):
    return pl.pallas_call(
        join_kernel,
        out_shape=jax.ShapeDtypeStruct((3 * gate.shape[0], BS, BS), BF),
        in_specs=[spec(pl.ANY)] * 3,
        out_specs=spec(pltpu.VMEM),
        scratch_shapes=[pltpu.SemaphoreType.DMA((3,))],
        name="join",
    )(gate, up, down)


def part_copies(shard, held, sems, share, parts, slot):
    here = pl.ds(slot * share, share)
    return [
        pltpu.make_async_copy(
            shard.at[pl.ds(part * share, share)], held.at[here, :, pl.ds(k * BS, BS)], sems.at[slot, k]
        )
        for k, part in enumerate(parts)
    ]


def start_parts(shards, held, sems, share, parts):
    for slot, shard in enumerate(shards):
        for copy in part_copies(shard, held, sems, share, parts, slot):
            copy.start()


def wait_parts(shards, held, sems, share, parts, slot):
    for copy in part_copies(shards[0], held, sems, share, parts, slot):
        copy.wait()


def shard_copies(shard, held_pair, held_down, sems, slot, share):
    here = pl.ds(slot * share, share)
    return [
        pltpu.make_async_copy(shard.at[pl.ds(0, share)], held_pair.at[here, :, pl.ds(0, BS)], sems.at[slot, 0]),
        pltpu.make_async_copy(shard.at[pl.ds(share, share)], held_pair.at[here, :, pl.ds(BS, BS)], sems.at[slot, 1]),
        pltpu.make_async_copy(shard.at[pl.ds(2 * share, share)], held_down.at[here], sems.at[slot, 2]),
    ]


def start_shards(shards, held_pair, held_down, sems, share):
    for slot, shard in enumerate(shards):
        for copy in shard_copies(shard, held_pair, held_down, sems, slot, share):
            copy.start()


def accumulate(share, at, table, rows, cols, normed, grad_out, shards, held_pair, held_down, sems, gate_up, back):
    def one_slot(slot, carry):
        for copy in shard_copies(shards[0], held_pair, held_down, sems, slot, share):
            copy.wait()
        base = table[at + slot] * share
        for j in range(share):
            row, col = rows[base + j], cols[base + j]
            gate_up[col] += mm(normed[:, lanes(row)], held_pair[slot * share + j])
            back[col] += mm_t(grad_out[:, lanes(row)], held_down[slot * share + j])
        return carry

    lax.fori_loop(0, len(shards), one_slot, 0)


def weight_grads(share, at, table, rows, cols, normed, grad_out, hidden, pre, grads, mine, other, sems):
    def stores(chip):
        return [
            pltpu.make_async_copy(grads.at[chip, 0], mine.at[chip], sems.at[chip, 0]),
            pltpu.make_async_copy(grads.at[chip, 1], other.at[chip], sems.at[chip, 1]),
        ]

    def one_chip(chip, carry):
        for flip in range(2):
            base = table[at + chip * 2 + flip] * share
            for j in range(share):
                row, col = rows[base + j], cols[base + j]
                both = mm_l(normed[:, lanes(row)], pre[col]).astype(BF)
                grads[chip, flip, j] = both[:, 0:BS]
                grads[chip, flip, share + j] = both[:, BS:]
                grads[chip, flip, 2 * share + j] = mm_l(hidden[col], grad_out[:, lanes(row)]).astype(BF)
            stores(chip)[flip].start()
        return carry

    lax.fori_loop(0, mine.shape[0], one_chip, 0)
    for chip in range(mine.shape[0]):
        for copy in stores(chip):
            copy.wait()


def early_kernel(share, count, *refs):
    table, rows, cols, normed, grad_out = refs[:5]
    shards = refs[5 : 5 + count]
    gate_up, back = refs[5 + count : 7 + count]
    held_pair, held_down, sems = refs[7 + count :]
    start_shards(shards, held_pair, held_down, sems, share)
    gate_up[...] = jnp.zeros_like(gate_up)
    back[...] = jnp.zeros_like(back)
    accumulate(
        share, AT_EARLY, table, rows, cols, normed, grad_out, shards, held_pair, held_down, sems, gate_up, back
    )


def early_call(table, rows, cols, normed, grad_out, shards, share, col_blocks):
    tokens = normed.shape[0]
    count = len(shards)
    return pl.pallas_call(
        functools.partial(early_kernel, share, count),
        out_shape=(
            jax.ShapeDtypeStruct((col_blocks, tokens, 2 * BS), F32),
            jax.ShapeDtypeStruct((col_blocks, tokens, BS), F32),
        ),
        in_specs=[spec(pltpu.SMEM)] * 3 + [spec(pltpu.VMEM)] * 2 + [spec(pl.ANY)] * count,
        out_specs=(spec(pltpu.VMEM), spec(pltpu.VMEM)),
        scratch_shapes=[
            pltpu.VMEM((count * share, BS, 2 * BS), BF),
            pltpu.VMEM((count * share, BS, BS), BF),
            pltpu.SemaphoreType.DMA((count, 3)),
        ],
        compiler_params=pltpu.CompilerParams(vmem_limit_bytes=VMEM_LIMIT),
        cost_estimate=pl.CostEstimate(flops=3 * 56 * 192 * 128 * 256, bytes_accessed=12_000_000, transcendentals=0),
        name="early",
    )(table, rows, cols, normed, grad_out, *shards)


def late_kernel(share, count, *refs):
    table, rows, cols, normed, grad_out, gate_up_in, back_in = refs[:7]
    shards = refs[7 : 7 + count]
    hidden, pre, mine, other = refs[7 + count : 11 + count]
    held_pair, held_down, gate_up, back, grads, sems, store_sems = refs[11 + count :]
    start_shards(shards, held_pair, held_down, sems, share)
    gate_up[...] = gate_up_in[...]
    back[...] = back_in[...]
    accumulate(
        share, AT_LATE, table, rows, cols, normed, grad_out, shards, held_pair, held_down, sems, gate_up, back
    )

    def activate(col, carry):
        gate = gate_up[col, :, 0:BS]
        up = gate_up[col, :, BS:]
        cot = back[col]
        sig = 1.0 / (1.0 + jnp.exp(-gate))
        act = gate * sig
        hidden[col] = (act * up).astype(BF)
        pre[col, :, 0:BS] = (cot * up * sig * (1.0 + gate * (1.0 - sig))).astype(BF)
        pre[col, :, BS:] = (cot * act).astype(BF)
        return carry

    lax.fori_loop(0, hidden.shape[0], activate, 0)
    weight_grads(
        share, AT_FIRST, table, rows, cols, normed, grad_out, hidden, pre, grads, mine, other, store_sems
    )


def late_call(table, rows, cols, normed, grad_out, gate_up, back, shards, share):
    col_blocks, tokens, _ = gate_up.shape
    count = len(shards)
    half = CHIPS // 2
    grads = jax.ShapeDtypeStruct((half, 3 * share, BS, BS), BF)
    return pl.pallas_call(
        functools.partial(late_kernel, share, count),
        out_shape=(
            jax.ShapeDtypeStruct((col_blocks, tokens, BS), BF),
            jax.ShapeDtypeStruct((col_blocks, tokens, 2 * BS), BF),
            grads,
            grads,
        ),
        in_specs=[spec(pltpu.SMEM)] * 3 + [spec(pltpu.VMEM)] * 4 + [spec(pl.ANY)] * count,
        out_specs=(spec(pltpu.VMEM), spec(pltpu.VMEM), spec(pl.ANY), spec(pl.ANY)),
        scratch_shapes=[
            pltpu.VMEM((count * share, BS, 2 * BS), BF),
            pltpu.VMEM((count * share, BS, BS), BF),
            pltpu.VMEM((col_blocks, tokens, 2 * BS), F32),
            pltpu.VMEM((col_blocks, tokens, BS), F32),
            pltpu.VMEM((half, 2, 3 * share, BS, BS), BF),
            pltpu.SemaphoreType.DMA((count, 3)),
            pltpu.SemaphoreType.DMA((half, 2)),
        ],
        compiler_params=pltpu.CompilerParams(vmem_limit_bytes=VMEM_LIMIT),
        cost_estimate=pl.CostEstimate(flops=6 * 56 * 192 * 128 * 256, bytes_accessed=20_000_000, transcendentals=0),
        name="late",
    )(table, rows, cols, normed, grad_out, gate_up, back, *shards)


def rest_kernel(share, table, rows, cols, normed, grad_out, hidden, pre, mine, other, grads, store_sems):
    weight_grads(
        share, AT_SECOND, table, rows, cols, normed, grad_out, hidden, pre, grads, mine, other, store_sems
    )


def rest_call(table, rows, cols, normed, grad_out, hidden, pre, share):
    half = CHIPS // 2
    grads = jax.ShapeDtypeStruct((half, 3 * share, BS, BS), BF)
    return pl.pallas_call(
        functools.partial(rest_kernel, share),
        out_shape=(grads, grads),
        in_specs=[spec(pltpu.SMEM)] * 3 + [spec(pltpu.VMEM)] * 4,
        out_specs=(spec(pl.ANY), spec(pl.ANY)),
        scratch_shapes=[
            pltpu.VMEM((half, 2, 3 * share, BS, BS), BF),
            pltpu.SemaphoreType.DMA((half, 2)),
        ],
        compiler_params=pltpu.CompilerParams(vmem_limit_bytes=VMEM_LIMIT),
        cost_estimate=pl.CostEstimate(flops=3 * 56 * 192 * 128 * 256, bytes_accessed=10_000_000, transcendentals=0),
        name="rest",
    )(table, rows, cols, normed, grad_out, hidden, pre)


def input_kernel(share, *refs):
    order, rows, cols, place, index, weights, pre, stats, gain = refs[:9]
    history = refs[9]
    shards = refs[10 : 10 + N_DP]
    pieces = refs[10 + N_DP : 14 + N_DP]
    small = refs[14 + N_DP]
    held, layers, total, s_wide, load_sems, layer_sems = refs[15 + N_DP :]
    tokens, width = total.shape
    start_parts(shards, held, load_sems, share, (0, 1))
    layer_copies = [
        pltpu.make_async_copy(history.at[index[slot]], layers.at[slot], layer_sems.at[slot]) for slot in range(4)
    ]
    for copy in layer_copies:
        copy.start()
    total[...] = jnp.zeros_like(total)

    def back_input(slot, carry):
        wait_parts(shards, held, load_sems, share, (0, 1), slot)
        base = order[slot] * share
        for j in range(share):
            row, col = rows[base + j], cols[base + j]
            total[:, lanes(row)] += mm_t(pre[col], held[slot * share + j])
        return carry

    lax.fori_loop(0, N_DP, back_input, 0)
    for copy in layer_copies:
        copy.wait()

    step = sign_of(place[0])
    offsets = (0, step, -step, 2)
    per_part = pieces[0].shape[2] // BS
    small[...] = jnp.zeros_like(small)
    lane = lax.broadcasted_iota(jnp.int32, (1, BS), 1)

    def finish(chunk, carry):
        here = pl.ds(pl.multiple_of(chunk * ROWS, ROWS), ROWS)
        stat = stats[here]
        scale = stat[:, 0:1]
        zero = jnp.zeros((ROWS, BS), F32)
        sums = [zero] * 4
        for way, piece in enumerate(pieces):
            x_there = (place[1] + offsets[way] + 2 * N_X) % N_X
            for part in range(N_YLO):
                half = (part + place[2]) % N_YLO
                for block in range(per_part):
                    row = (x_there * N_YLO + half) * per_part + block
                    where = lanes(row)
                    value = total[here, where]
                    piece[part, here, block * BS : (block + 1) * BS] = value.astype(BF)
                    scaled = value * gain[:, where]
                    mixed = zero
                    for slot in range(4):
                        layer = layers[slot, here, where].astype(F32)
                        sums[slot] = sums[slot] + scaled * layer
                        mixed = mixed + weights[slot] * layer
                    small[pl.ds(row, 1), :] += jnp.sum(value * mixed * scale, axis=0, keepdims=True)
        alphas = [jnp.sum(total_sum, axis=1, keepdims=True) for total_sum in sums]
        s_col = sum(weights[slot] * alphas[slot] for slot in range(4))
        s_wide[here] = jnp.broadcast_to(s_col, (ROWS, BS))
        depth = jnp.zeros((1, BS), F32)
        for slot in range(4):
            per_token = (
                scale * alphas[slot]
                - scale * scale * scale * stat[:, 1 + slot : 2 + slot] * s_col / width
                + stat[:, 5 + slot : 6 + slot] / N_TENSOR
            )
            depth = jnp.where(lane == slot, jnp.sum(per_token, axis=0, keepdims=True), depth)
        small[width // BS : width // BS + 1, :] += depth
        return carry

    lax.fori_loop(0, tokens // ROWS, finish, 0)
    s_row = jnp.transpose(s_wide[...])[0:1]
    for piece in pieces:
        for part in range(N_YLO):
            piece[part, tokens:] = jnp.zeros((EXTRA, piece.shape[2]), BF)
            for block in range(2):
                size = min(BS, tokens - block * BS)
                lead = jnp.broadcast_to(s_row[:, block * BS : block * BS + size], (EXTRA, size))
                piece[part, tokens:, block * BS : block * BS + size] = lead.astype(BF)


def input_call(order, rows, cols, place, depth_index, depth_weights, pre, stats, gain, history, shards, share):
    tokens = pre.shape[1]
    width = history.shape[2]
    piece = jax.ShapeDtypeStruct((N_YLO, tokens + EXTRA, width // N_TENSOR), BF)
    return pl.pallas_call(
        functools.partial(input_kernel, share),
        out_shape=(piece,) * N_X + (jax.ShapeDtypeStruct((width // BS + 8, BS), F32),),
        in_specs=[spec(pltpu.SMEM)] * 6 + [spec(pltpu.VMEM)] * 3 + [spec(pl.ANY)] * (N_DP + 1),
        out_specs=(spec(pltpu.VMEM),) * (N_X + 1),
        scratch_shapes=[
            pltpu.VMEM((N_DP * share, BS, 2 * BS), BF),
            pltpu.VMEM((4, tokens, width), BF),
            pltpu.VMEM((tokens, width), F32),
            pltpu.VMEM((tokens, BS), F32),
            pltpu.SemaphoreType.DMA((N_DP, 2)),
            pltpu.SemaphoreType.DMA((4,)),
        ],
        compiler_params=pltpu.CompilerParams(vmem_limit_bytes=VMEM_LIMIT),
        cost_estimate=pl.CostEstimate(flops=2 * 112 * 192 * 128 * 256, bytes_accessed=20_000_000, transcendentals=0),
        name="input_grad",
    )(order, rows, cols, place, depth_index, depth_weights, pre, stats, gain.reshape(1, width), history, *shards)


def output_kernel(share, *refs):
    order, rows, cols, place, hidden = refs[:5]
    shards = refs[5 : 5 + N_DP]
    pieces = refs[5 + N_DP : 9 + N_DP]
    held, total, load_sems = refs[9 + N_DP :]
    start_parts(shards, held, load_sems, share, (2,))
    total[...] = jnp.zeros_like(total)

    def forward(slot, carry):
        wait_parts(shards, held, load_sems, share, (2,), slot)
        base = order[slot] * share
        for j in range(share):
            row, col = rows[base + j], cols[base + j]
            total[:, lanes(row)] += mm(hidden[col], held[slot * share + j])
        return carry

    lax.fori_loop(0, N_DP, forward, 0)
    step = sign_of(place[0])
    offsets = (0, step, -step, 2)
    for way, piece in enumerate(pieces):
        x_there = (place[1] + offsets[way] + 2 * N_X) % N_X
        for part in range(N_YLO):
            half = (part + place[2]) % N_YLO
            size = piece.shape[2]
            piece[part] = total[:, lanes(x_there * N_YLO + half, size)].astype(BF)


def output_call(order, rows, cols, place, hidden, shards, share, width):
    tokens = hidden.shape[1]
    piece = jax.ShapeDtypeStruct((N_YLO, tokens, width // N_TENSOR), BF)
    return pl.pallas_call(
        functools.partial(output_kernel, share),
        out_shape=(piece,) * N_X,
        in_specs=[spec(pltpu.SMEM)] * 4 + [spec(pltpu.VMEM)] + [spec(pl.ANY)] * N_DP,
        out_specs=(spec(pltpu.VMEM),) * N_X,
        scratch_shapes=[
            pltpu.VMEM((N_DP * share, BS, BS), BF),
            pltpu.VMEM((tokens, width), F32),
            pltpu.SemaphoreType.DMA((N_DP, 1)),
        ],
        compiler_params=pltpu.CompilerParams(vmem_limit_bytes=VMEM_LIMIT),
        cost_estimate=pl.CostEstimate(flops=112 * 192 * 128 * 256, bytes_accessed=10_000_000, transcendentals=0),
        name="output",
    )(order, rows, cols, place, hidden, *shards)


def add(*values):
    return sum(v.astype(F32) for v in values)


def reduce_tensor(pieces):
    own, to_a, to_b, far = pieces
    near = add(to_a, over_tensor(far, "a")).astype(BF)
    total = add(own, over_tensor(near, "a"), over_tensor(to_b, "b"))
    return add(total[0], over_tensor(total[1].astype(BF), "y"))


def reduce_small(small):
    for kinds in (("z1", "z2", "z3"), ("c", "y", "yc")):
        one, two, three = [over_dp(small, kind) for kind in kinds]
        small = (small + one) + (two + three)
    for kind in ("1", "2", "y"):
        small = small + over_tensor(small, kind)
    return small


def per_device(
    history,
    depth_weights,
    depth_index,
    gain,
    gate_blocks,
    up_blocks,
    down_blocks,
    block_ids,
    grad_out,
):
    tokens, width = grad_out.shape
    share = gate_blocks.shape[0]
    col_blocks = 14
    share_width = width // N_TENSOR
    dp = lax.axis_index("dp")
    tensor = lax.axis_index("tensor")
    core = dp % N_CORE
    share_start = tensor * share_width

    ahead = jnp.array([AHEAD[chip] for chip, _ in TABLE], jnp.int32)
    turn = jnp.array([TURN[chip] for chip, _ in TABLE], jnp.int32)
    flip = jnp.array([f for _, f in TABLE], jnp.int32)
    there = (core + flip) % N_CORE
    table = (
        ((dp // (N_Y * N_CORE) + ahead * sign_of(there) + 2 * N_Z) % N_Z) * (N_Y * N_CORE)
        + ((dp // N_CORE + turn) % N_Y) * N_CORE
        + there
    ).astype(jnp.int32)
    rows, cols = block_ids[:, 0], block_ids[:, 1]
    where = jnp.arange(4, dtype=jnp.int32)
    place = jnp.where(where == 0, core, jnp.where(where == 1, tensor // N_YLO, tensor % N_YLO)).astype(jnp.int32)

    got = {}
    own = join_call(gate_blocks, up_blocks, down_blocks)
    got[OWN, 0] = own
    got[A1, 0] = over_dp(own, "a")
    got[B1, 0] = over_dp(own, "b")
    got[YY, 0] = over_dp(own, "y")
    normed, stats, kept = norm_call(depth_index, depth_weights, history, grad_out, gain)
    got[A2, 0] = over_dp(got[A1, 0], "a")
    got[YA, 0] = over_dp(got[YY, 0], "a")
    got[YB, 0] = over_dp(got[YY, 0], "b")
    got[Y2, 0] = over_dp(got[A2, 0], "y")
    for chip in range(CHIPS):
        got[chip, 1] = over_dp(got[chip, 0], "c")

    gate_up, back = early_call(
        table, rows, cols, normed, grad_out, [got[key] for key in EARLY], share, col_blocks
    )
    hidden, pre, mine1, other1 = late_call(
        table, rows, cols, normed, grad_out, gate_up, back, [got[key] for key in LATE], share
    )
    arrived1 = over_dp(other1, "c")
    mine2, other2 = rest_call(table, rows, cols, normed, grad_out, hidden, pre, share)
    arrived2 = over_dp(other2, "c")
    part = {}
    for k in range(CHIPS // 2):
        part[SECOND[k]] = add(mine2[k], arrived2[k])
    far_y = over_dp(add(mine1[0], arrived1[0]).astype(BF), "y")
    across_a = over_dp(add(mine1[1], arrived1[1]).astype(BF), "a")
    both_b = over_dp(add(mine1[2:4], arrived1[2:4]).astype(BF), "b")
    across_b, near_b = both_b[0], both_b[1]

    shards = [got[key] for key in EARLY + LATE]
    *back_pieces, small = input_call(
        table, rows, cols, place, depth_index, depth_weights, pre, stats, gain, history, shards, share
    )
    out_pieces = output_call(table, rows, cols, place, hidden, shards, share, width)

    mine_y, arrived_y, across_a, across_b = lax.optimization_barrier((mine2, arrived2, across_a, across_b))
    at = SECOND.index(YY)
    part[YY] = add(mine_y[at], arrived_y[at])
    far = add(part[A2], far_y).astype(BF)
    near = add(part[B1], over_dp(far, "a")).astype(BF)
    across = over_dp(add(part[YY], across_a, across_b).astype(BF), "y")
    near_a = over_dp(near, "a")
    own1, own2 = mine2[SECOND.index(OWN)], arrived2[SECOND.index(OWN)]
    block_grads = [
        add(*[v[k * share : (k + 1) * share] for v in (own1, own2, near_a, near_b, across)]) for k in range(3)
    ]

    back = reduce_tensor(back_pieces)
    ffn = reduce_tensor(out_pieces)
    small = reduce_small(small)

    mixed = lax.dynamic_slice_in_dim(kept, share_start, share_width, 1)
    layer_out = (mixed + ffn).astype(BF)

    scale = stats[:, 0:1]
    gain_share = lax.dynamic_slice_in_dim(gain, share_start, share_width, 0)
    cot = lax.dynamic_slice_in_dim(grad_out, share_start, share_width, 1).astype(F32)
    s_col = back[tokens, 0:tokens].reshape(tokens, 1)
    grad_mixed = cot + scale * gain_share * back[0:tokens] - mixed * (scale * scale * scale) * (s_col / width)

    return (
        layer_out,
        grad_mixed,
        block_grads[0],
        block_grads[1],
        block_grads[2],
        small[width // BS, 0:4],
        lax.dynamic_slice_in_dim(small, share_start // BS, share_width // BS, 0).reshape(share_width),
    )


def solution(mesh):
    placed = (
        P(None, "dp", None),
        P(),
        P(),
        P(),
        P(("tensor", "dp"), None, None),
        P(("tensor", "dp"), None, None),
        P(("tensor", "dp"), None, None),
        P("tensor", None),
        P("dp", None),
    )

    return jax.shard_map(
        per_device,
        mesh=mesh,
        in_specs=placed,
        out_specs=(
            P("dp", "tensor"),
            P("dp", "tensor"),
            P(("tensor", "dp"), None, None),
            P(("tensor", "dp"), None, None),
            P(("tensor", "dp"), None, None),
            P(),
            P("tensor"),
        ),
        check_vma=False,
    )
```

profile of v0, /device:TPU:0, one launch (start us, length us, event | category | flops | bytes accessed | tf_op | source)
XLA Modules:
  0.0 215.0 jit_solution(16310033929619979578)
XLA Ops:
  0.6 2.0 join.1.refs_5_.refs_10_
  2.7 2.1 collective-permute-start.1
  4.8 2.2 %collective-permute-start.3 = (bf16[21,128,128]{2,1,0:T(8,128)(2,1)}, bf16[21,128,128]{2,1,0:T(8,128)(2,1)S(1)}, u32[]{:S(2)}, u32[]{:S(2)}) collective-permute-start(bf16[21,128,128]{2,1,0:T(8,128)(2,1)} %join.1.refs_5_.refs_10_), channel_id=1, source_target_pairs={{0,96},{8,40},{16,112},{24,56},{32,0},{40,72},{48,16},{56,88},{64,... | collective-permute-start | bytes 2064392 | tf_op jit(solution)/shard_map/ppermute | solution.py:89
  7.0 3.2 %collective-permute-start.5 = (bf16[21,128,128]{2,1,0:T(8,128)(2,1)}, bf16[21,128,128]{2,1,0:T(8,128)(2,1)S(1)}, u32[]{:S(2)}, u32[]{:S(2)}) collective-permute-start(bf16[21,128,128]{2,1,0:T(8,128)(2,1)} %join.1.refs_5_.refs_10_), channel_id=1, source_target_pairs={{0,16},{8,24},{16,0},{24,8},{32,48},{40,56},{48,32},{56,40},{64,80... | collective-permute-start | bytes 2064392 | tf_op jit(solution)/shard_map/ppermute | solution.py:89
  10.2 11.4 %collective-permute-done.1.refs_7_.refs_12_ = bf16[21,128,128]{2,1,0:T(8,128)(2,1)S(1)} collective-permute-done((bf16[21,128,128]{2,1,0:T(8,128)(2,1)}, bf16[21,128,128]{2,1,0:T(8,128)(2,1)S(1)}, u32[]{:S(2)}, u32[]{:S(2)}) %collective-permute-start.1) | collective-permute-done | bytes 688160 | tf_op jit(solution)/shard_map/ppermute | solution.py:89
  21.6 0.7 collective-permute-start.7
  22.3 1.8 collective-permute-start.2
  24.2 1.3 collective-permute-done.5.refs_11_.refs_16_
  25.5 3.2 %collective-permute-start.11 = (bf16[21,128,128]{2,1,0:T(8,128)(2,1)S(1)}, bf16[21,128,128]{2,1,0:T(8,128)(2,1)}, u32[]{:S(2)}, u32[]{:S(2)}) collective-permute-start(bf16[21,128,128]{2,1,0:T(8,128)(2,1)S(1)} %collective-permute-done.5.refs_11_.refs_16_), channel_id=1, source_target_pairs={{0,96},{8,40},{16,112},{24,56},{32,0},{40,72},{48,16},{56,88},{64,... | collective-permute-start | bytes 2064392 | tf_op jit(solution)/shard_map/ppermute | solution.py:89
  28.8 7.1 %collective-permute-done.7.refs_7_.refs_13_.refs_18_ = bf16[21,128,128]{2,1,0:T(8,128)(2,1)} collective-permute-done((bf16[21,128,128]{2,1,0:T(8,128)(2,1)S(1)}, bf16[21,128,128]{2,1,0:T(8,128)(2,1)}, u32[]{:S(2)}, u32[]{:S(2)}) %collective-permute-start.7) | collective-permute-done | bytes 688160 | tf_op jit(solution)/shard_map/ppermute | solution.py:89
  35.9 3.2 %collective-permute-start.13 = (bf16[21,128,128]{2,1,0:T(8,128)(2,1)}, bf16[21,128,128]{2,1,0:T(8,128)(2,1)}, u32[]{:S(2)}, u32[]{:S(2)}) collective-permute-start(bf16[21,128,128]{2,1,0:T(8,128)(2,1)} %collective-permute-done.7.refs_7_.refs_13_.refs_18_), channel_id=1, source_target_pairs={{0,16},{8,24},{16,0},{24,8},{32,48},{40,56},{48,32},{56,40},{64,80... | collective-permute-start | bytes 2064392 | tf_op jit(solution)/shard_map/ppermute | solution.py:89
  39.6 8.9 %collective-permute-done.9.refs_9_.refs_15_.refs_20_ = bf16[21,128,128]{2,1,0:T(8,128)(2,1)} collective-permute-done((bf16[21,128,128]{2,1,0:T(8,128)(2,1)S(1)}, bf16[21,128,128]{2,1,0:T(8,128)(2,1)}, u32[]{:S(2)}, u32[]{:S(2)}) %collective-permute-start.9) | collective-permute-done | bytes 688160 | tf_op jit(solution)/shard_map/ppermute | solution.py:89
  49.1 4.1 %collective-permute-done.13.refs_13_.refs_19_.refs_24_ = bf16[21,128,128]{2,1,0:T(8,128)(2,1)} collective-permute-done((bf16[21,128,128]{2,1,0:T(8,128)(2,1)}, bf16[21,128,128]{2,1,0:T(8,128)(2,1)}, u32[]{:S(2)}, u32[]{:S(2)}) %collective-permute-start.13) | collective-permute-done | bytes 688160 | tf_op jit(solution)/shard_map/ppermute | solution.py:89
  53.2 11.7 %norm.1 = (bf16[192,4096]{1,0:T(8,128)(2,1)}, f32[192,128]{1,0:T(8,128)}, f32[192,4096]{1,0:T(8,128)}) custom-call(s32[4]{0:T(128)} %refs_4_.5, f32[4]{0:T(128)} %refs_5_.1, bf16[4,192,4096]{2,1,0:T(8,128)(2,1)} %refs_9_.1, bf16[4,192,4096]{2,1,0:T(8,128)(2,1)} %refs_9_.1, bf16[4,192,4096]{2,1,0:T(8,128)(2,1)} %refs_9_.1, bf16[4,192,4096]{2,1,0:T(8,128)(2,1)} %refs_9_.1, ...), custom_call_target="tpu_custom_call" | custom-call | flops 23592960 | bytes 9437184 | tf_op jit(solution)/shard_map/norm/pallas_call | solution.py:155
  66.1 8.9 %early.1 = (f32[14,192,256]{2,1,0:T(8,128)}, f32[14,192,128]{2,1,0:T(8,128)}) custom-call(s32[32]{0:T(128)} %fusion.22.refs_0_.table, s32[112]{0:T(128)} %get-tuple-element.65.refs_1_.rows, s32[112]{0:T(128)} %get-tuple-element.64.refs_2_.cols, bf16[192,4096]{1,0:T(8,128)(2,1)} %get-tuple-element.32.refs_3_.normed, bf16[192,4096]{1,0:T(8,128)(2,1)} %grad_out.3, ...), custom_call_target="tpu_custom_call" | custom-call | flops 1056964608 | bytes 12000000 | tf_op jit(solution)/shard_map/early/pallas_call | solution.py:297
  75.0 14.2 %late.1 = (bf16[14,192,128]{2,1,0:T(8,128)(2,1)}, bf16[14,192,256]{2,1,0:T(8,128)(2,1)}, bf16[4,21,128,128]{3,2,1,0:T(8,128)(2,1)}, bf16[4,21,128,128]{3,2,1,0:T(8,128)(2,1)}) custom-call(s32[32]{0:T(128)} %fusion.22.refs_0_.table, s32[112]{0:T(128)} %get-tuple-element.65.refs_1_.rows, s32[112]{0:T(128)} %get-tuple-element.64.refs_2_.cols, ...), custom_call_target="tpu_custom_call" | custom-call | flops 2113929216 | bytes 20000000 | tf_op jit(solution)/shard_map/late/pallas_call | solution.py:350
  90.3 14.8 %input_grad.1 = (bf16[2,208,512]{2,1,0:T(8,128)(2,1)}, bf16[2,208,512]{2,1,0:T(8,128)(2,1)}, bf16[2,208,512]{2,1,0:T(8,128)(2,1)}, bf16[2,208,512]{2,1,0:T(8,128)(2,1)}, f32[40,128]{1,0:T(8,128)}) custom-call(s32[32]{0:T(128)} %fusion.22.refs_0_.table, s32[112]{0:T(128)} %get-tuple-element.65.refs_1_.rows, s32[112]{0:T(128)} %get-tuple-element.64.refs_2_.cols, ...), custom_call_target="tpu_custom_call" | custom-call | flops 1409286144 | bytes 20000000 | tf_op jit(solution)/shard_map/input_grad/pallas_call | solution.py:484
  105.0 0.9 collective-permute-start.32
  105.9 3.0 %collective-permute-start.33 = (f32[40,128]{1,0:T(8,128)}, f32[40,128]{1,0:T(8,128)S(1)}, u32[]{:S(2)}, u32[]{:S(2)}) collective-permute-start(f32[40,128]{1,0:T(8,128)} %get-tuple-element.54), channel_id=1, source_target_pairs={{0,96},{8,104},{16,112},{24,120},{32,64},{40,72},{48,80},{56,88},{... | collective-permute-start | bytes 61448 | tf_op jit(solution)/shard_map/ppermute | solution.py:89
  109.0 0.8 collective-permute-start.31
  109.8 6.4 %rest.1 = (bf16[4,21,128,128]{3,2,1,0:T(8,128)(2,1)}, bf16[4,21,128,128]{3,2,1,0:T(8,128)(2,1)}) custom-call(s32[32]{0:T(128)} %fusion.22.refs_0_.table, s32[112]{0:T(128)} %get-tuple-element.65.refs_1_.rows, s32[112]{0:T(128)} %get-tuple-element.64.refs_2_.cols, bf16[192,4096]{1,0:T(8,128)(2,1)} %get-tuple-element.32.refs_3_.normed, ...), custom_call_target="tpu_custom_call" | custom-call | flops 1056964608 | bytes 10000000 | tf_op jit(solution)/shard_map/rest/pallas_call | solution.py:384
  116.3 3.3 %collective-permute-start.35 = (f32[40,128]{1,0:T(8,128)S(1)}, f32[40,128]{1,0:T(8,128)S(1)}, u32[]{:S(2)}, u32[]{:S(2)}) collective-permute-start(f32[40,128]{1,0:T(8,128)S(1)} %add_add_fusion.1), channel_id=1, source_target_pairs={{0,16},{8,24},{16,0},{24,8},{32,48},{40,56},{48,32},{56,40},{64,80... | collective-permute-start | bytes 61448 | tf_op jit(solution)/shard_map/ppermute | solution.py:89
  120.0 1.6 collective-permute-done.35
  121.6 2.6 %collective-permute-done.36 = f32[40,128]{1,0:T(8,128)S(1)} collective-permute-done((f32[40,128]{1,0:T(8,128)S(1)}, f32[40,128]{1,0:T(8,128)S(1)}, u32[]{:S(2)}, u32[]{:S(2)}) %collective-permute-start.36) | collective-permute-done | bytes 20512 | tf_op jit(solution)/shard_map/ppermute | solution.py:89
  124.3 1.6 collective-permute-start.37
  125.8 2.3 %collective-permute-done.37 = f32[40,128]{1,0:T(8,128)S(1)} collective-permute-done((f32[40,128]{1,0:T(8,128)S(1)}, f32[40,128]{1,0:T(8,128)S(1)}, u32[]{:S(2)}, u32[]{:S(2)}) %collective-permute-start.37) | collective-permute-done | bytes 20512 | tf_op jit(solution)/shard_map/ppermute | solution.py:93
  128.2 2.9 %collective-permute-start.38 = (f32[40,128]{1,0:T(8,128)S(1)}, f32[40,128]{1,0:T(8,128)S(1)}, u32[]{:S(2)}, u32[]{:S(2)}) collective-permute-start(f32[40,128]{1,0:T(8,128)S(1)} %add.266), channel_id=1, source_target_pairs={{0,4},{1,5},{2,6},{3,7},{4,0},{5,1},{6,2},{7,3},{8,12},{9,13},{10,... | collective-permute-start | bytes 61448 | tf_op jit(solution)/shard_map/ppermute | solution.py:93
  131.1 8.3 %output.1 = (bf16[2,192,512]{2,1,0:T(8,128)(2,1)}, bf16[2,192,512]{2,1,0:T(8,128)(2,1)}, bf16[2,192,512]{2,1,0:T(8,128)(2,1)}, bf16[2,192,512]{2,1,0:T(8,128)(2,1)}) custom-call(s32[32]{0:T(128)} %fusion.22.refs_0_.table, s32[112]{0:T(128)} %get-tuple-element.65.refs_1_.rows, s32[112]{0:T(128)} %get-tuple-element.64.refs_2_.cols, ...), custom_call_target="tpu_custom_call" | custom-call | flops 704643072 | bytes 10000000 | tf_op jit(solution)/shard_map/output/pallas_call | solution.py:533
  140.1 0.8 collective-permute-start.39
  141.1 0.8 dynamic_slice.14
  141.8 2.6 %collective-permute-start.21 = (bf16[2,208,512]{2,1,0:T(8,128)(2,1)}, bf16[2,208,512]{2,1,0:T(8,128)(2,1)S(1)}, u32[]{:S(2)}, u32[]{:S(2)}) collective-permute-start(bf16[2,208,512]{2,1,0:T(8,128)(2,1)} %get-tuple-element.45), channel_id=1, source_target_pairs={{0,6},{1,7},{2,0},{3,1},{4,2},{5,3},{6,4},{7,5},{8,10},{9,11},{10,... | collective-permute-start | bytes 1277960 | tf_op jit(solution)/shard_map/ppermute | solution.py:93
  145.6 7.4 %collective-permute-done.15 = bf16[2,192,512]{2,1,0:T(8,128)(2,1)} collective-permute-done((bf16[2,192,512]{2,1,0:T(8,128)(2,1)}, bf16[2,192,512]{2,1,0:T(8,128)(2,1)}, u32[]{:S(2)}, u32[]{:S(2)}) %collective-permute-start.15) | collective-permute-done | bytes 393248 | tf_op jit(solution)/shard_map/ppermute | solution.py:93
  153.0 1.2 add_convert_fusion.4
  154.2 7.8 %collective-permute-done.19 = bf16[2,208,512]{2,1,0:T(8,128)(2,1)S(1)} collective-permute-done((bf16[2,208,512]{2,1,0:T(8,128)(2,1)}, bf16[2,208,512]{2,1,0:T(8,128)(2,1)S(1)}, u32[]{:S(2)}, u32[]{:S(2)}) %collective-permute-start.19) | collective-permute-done | bytes 426016 | tf_op jit(solution)/shard_map/ppermute | solution.py:93
  162.1 2.4 %add_convert_fusion = bf16[2,21,128,128]{3,2,1,0:T(8,128)(2,1)S(1)} fusion(bf16[4,21,128,128]{3,2,1,0:T(8,128)(2,1)} %collective-permute-done.24, bf16[4,21,128,128]{3,2,1,0:T(8,128)(2,1)} %get-tuple-element.48), kind=kLoop, calls=%fused_computation | loop fusion | flops 2752512 | bytes 4128768 | tf_op jit(solution)/shard_map/convert_element_type | solution.py:630
  164.6 2.7 %collective-permute-start.28 = (bf16[2,21,128,128]{3,2,1,0:T(8,128)(2,1)S(1)}, bf16[2,21,128,128]{3,2,1,0:T(8,128)(2,1)S(1)}, u32[]{:S(2)}, u32[]{:S(2)}) collective-permute-start(bf16[2,21,128,128]{3,2,1,0:T(8,128)(2,1)S(1)} %add_convert_fusion), channel_id=1, source_target_pairs={{0,96},{8,40},{16,112},{24,56},{32,0},{40,72},{48,16},{56,88},{64,... | collective-permute-start | bytes 4128776 | tf_op jit(solution)/shard_map/ppermute | solution.py:89
  167.3 1.8 fusion.4
  169.2 1.8 collective-permute-done.16
  171.2 1.7 collective-permute-start.18
  172.9 5.7 %collective-permute-done.20 = bf16[2,208,512]{2,1,0:T(8,128)(2,1)S(1)} collective-permute-done((bf16[2,208,512]{2,1,0:T(8,128)(2,1)S(1)}, bf16[2,208,512]{2,1,0:T(8,128)(2,1)S(1)}, u32[]{:S(2)}, u32[]{:S(2)}) %collective-permute-start.20) | collective-permute-done | bytes 426016 | tf_op jit(solution)/shard_map/ppermute | solution.py:93
  178.8 9.7 %collective-permute-done.25 = bf16[21,128,128]{2,1,0:T(8,128)(2,1)S(1)} collective-permute-done((bf16[21,128,128]{2,1,0:T(8,128)(2,1)S(1)}, bf16[21,128,128]{2,1,0:T(8,128)(2,1)S(1)}, u32[]{:S(2)}, u32[]{:S(2)}) %collective-permute-start.25) | collective-permute-done | bytes 688160 | tf_op jit(solution)/shard_map/ppermute | solution.py:89
  188.8 1.3 collective-permute-start.26
  190.3 3.1 %collective-permute-done.28 = bf16[2,21,128,128]{3,2,1,0:T(8,128)(2,1)S(1)} collective-permute-done((bf16[2,21,128,128]{3,2,1,0:T(8,128)(2,1)S(1)}, bf16[2,21,128,128]{3,2,1,0:T(8,128)(2,1)S(1)}, u32[]{:S(2)}, u32[]{:S(2)}) %collective-permute-start.28) | collective-permute-done | bytes 1376288 | tf_op jit(solution)/shard_map/ppermute | solution.py:89
  194.0 7.1 %collective-permute-done.26 = bf16[21,128,128]{2,1,0:T(8,128)(2,1)S(1)} collective-permute-done((bf16[21,128,128]{2,1,0:T(8,128)(2,1)S(1)}, bf16[21,128,128]{2,1,0:T(8,128)(2,1)S(1)}, u32[]{:S(2)}, u32[]{:S(2)}) %collective-permute-start.26) | collective-permute-done | bytes 688160 | tf_op jit(solution)/shard_map/ppermute | solution.py:89
  201.6 2.0 fusion.11
  203.6 5.8 %collective-permute-done.30 = bf16[21,128,128]{2,1,0:T(8,128)(2,1)S(1)} collective-permute-done((bf16[21,128,128]{2,1,0:T(8,128)(2,1)S(1)}, bf16[21,128,128]{2,1,0:T(8,128)(2,1)S(1)}, u32[]{:S(2)}, u32[]{:S(2)}) %collective-permute-start.30) | collective-permute-done | bytes 688160 | tf_op jit(solution)/shard_map/ppermute | solution.py:89
  209.4 4.2 %collective-permute-done.27 = bf16[21,128,128]{2,1,0:T(8,128)(2,1)S(1)} collective-permute-done((bf16[21,128,128]{2,1,0:T(8,128)(2,1)S(1)}, bf16[21,128,128]{2,1,0:T(8,128)(2,1)S(1)}, u32[]{:S(2)}, u32[]{:S(2)}) %collective-permute-start.27) | collective-permute-done | bytes 688160 | tf_op jit(solution)/shard_map/ppermute | solution.py:89
  213.6 1.4 fusion.6
  (101 shorter events, 8.0 us)
Async XLA Ops:
  2.7 18.9 %collective-permute-start.1 = (bf16[21,128,128]{2,1,0:T(8,128)(2,1)}, bf16[21,128,128]{2,1,0:T(8,128)(2,1)S(1)}, u32[]{:S(2)}, u32[]{:S(2)}) collective-permute-start(bf16[21,128,128]{2,1,0:T(8,128)(2,1)} %join.1.refs_5_.refs_10_), channel_id=1, source_target_pairs={{0,32},{8,104},{16,48},{24,120},{32,64},{40,8},{48,80},{56,24},{64... | collective-permute-start | bytes 2064392 | tf_op jit(solution)/shard_map/ppermute | solution.py:89
  4.8 19.3 %collective-permute-start.3 = (bf16[21,128,128]{2,1,0:T(8,128)(2,1)}, bf16[21,128,128]{2,1,0:T(8,128)(2,1)S(1)}, u32[]{:S(2)}, u32[]{:S(2)}) collective-permute-start(bf16[21,128,128]{2,1,0:T(8,128)(2,1)} %join.1.refs_5_.refs_10_), channel_id=1, source_target_pairs={{0,96},{8,40},{16,112},{24,56},{32,0},{40,72},{48,16},{56,88},{64,... | collective-permute-start | bytes 2064392 | tf_op jit(solution)/shard_map/ppermute | solution.py:89
  7.0 18.5 %collective-permute-start.5 = (bf16[21,128,128]{2,1,0:T(8,128)(2,1)}, bf16[21,128,128]{2,1,0:T(8,128)(2,1)S(1)}, u32[]{:S(2)}, u32[]{:S(2)}) collective-permute-start(bf16[21,128,128]{2,1,0:T(8,128)(2,1)} %join.1.refs_5_.refs_10_), channel_id=1, source_target_pairs={{0,16},{8,24},{16,0},{24,8},{32,48},{40,56},{48,32},{56,40},{64,80... | collective-permute-start | bytes 2064392 | tf_op jit(solution)/shard_map/ppermute | solution.py:89
  10.2 15.4 %collective-permute-start = (bf16[21,128,128]{2,1,0:T(8,128)(2,1)}, bf16[21,128,128]{2,1,0:T(8,128)(2,1)S(1)}, u32[]{:S(2)}, u32[]{:S(2)}) collective-permute-start(bf16[21,128,128]{2,1,0:T(8,128)(2,1)} %join.1.refs_5_.refs_10_), channel_id=1, source_target_pairs={{0,8},{8,0},{16,24},{24,16},{32,40},{40,32},{48,56},{56,48},{64,72... | collective-permute-start | bytes 2064392 | tf_op jit(solution)/shard_map/ppermute | solution.py:89
  21.6 43.4 %copy-start = (bf16[21,128,128]{2,1,0:T(8,128)(2,1)}, bf16[21,128,128]{2,1,0:T(8,128)(2,1)S(1)}, u32[]{:S(2)}) copy-start(bf16[21,128,128]{2,1,0:T(8,128)(2,1)S(1)} %collective-permute-done.1.refs_7_.refs_12_) | copy-start | bytes 2064388
  21.6 14.3 %collective-permute-start.7 = (bf16[21,128,128]{2,1,0:T(8,128)(2,1)S(1)}, bf16[21,128,128]{2,1,0:T(8,128)(2,1)}, u32[]{:S(2)}, u32[]{:S(2)}) collective-permute-start(bf16[21,128,128]{2,1,0:T(8,128)(2,1)S(1)} %collective-permute-done.1.refs_7_.refs_12_), channel_id=1, source_target_pairs={{0,32},{8,104},{16,48},{24,120},{32,64},{40,8},{48,80},{56,24},{64... | collective-permute-start | bytes 2064392 | tf_op jit(solution)/shard_map/ppermute | solution.py:89
  22.3 16.9 %collective-permute-start.2 = (bf16[21,128,128]{2,1,0:T(8,128)(2,1)S(1)}, bf16[21,128,128]{2,1,0:T(8,128)(2,1)S(1)}, u32[]{:S(2)}, u32[]{:S(2)}) collective-permute-start(bf16[21,128,128]{2,1,0:T(8,128)(2,1)S(1)} %collective-permute-done.1.refs_7_.refs_12_), channel_id=1, source_target_pairs={{0,8},{8,0},{16,24},{24,16},{32,40},{40,32},{48,56},{56,48},{64,72... | collective-permute-start | bytes 2064392 | tf_op jit(solution)/shard_map/ppermute | solution.py:89
  24.1 40.8 %copy-start.1 = (bf16[21,128,128]{2,1,0:T(8,128)(2,1)}, bf16[21,128,128]{2,1,0:T(8,128)(2,1)S(1)}, u32[]{:S(2)}) copy-start(bf16[21,128,128]{2,1,0:T(8,128)(2,1)S(1)} %collective-permute-done.3.refs_9_.refs_14_) | copy-start | bytes 2064388
  24.1 15.0 %collective-permute-start.4 = (bf16[21,128,128]{2,1,0:T(8,128)(2,1)S(1)}, bf16[21,128,128]{2,1,0:T(8,128)(2,1)S(1)}, u32[]{:S(2)}, u32[]{:S(2)}) collective-permute-start(bf16[21,128,128]{2,1,0:T(8,128)(2,1)S(1)} %collective-permute-done.3.refs_9_.refs_14_), channel_id=1, source_target_pairs={{0,8},{8,0},{16,24},{24,16},{32,40},{40,32},{48,56},{56,48},{64,72... | collective-permute-start | bytes 2064392 | tf_op jit(solution)/shard_map/ppermute | solution.py:89
  25.5 39.4 %copy-start.2 = (bf16[21,128,128]{2,1,0:T(8,128)(2,1)}, bf16[21,128,128]{2,1,0:T(8,128)(2,1)S(1)}, u32[]{:S(2)}) copy-start(bf16[21,128,128]{2,1,0:T(8,128)(2,1)S(1)} %collective-permute-done.5.refs_11_.refs_16_) | copy-start | bytes 2064388
  25.5 23.1 %collective-permute-start.9 = (bf16[21,128,128]{2,1,0:T(8,128)(2,1)S(1)}, bf16[21,128,128]{2,1,0:T(8,128)(2,1)}, u32[]{:S(2)}, u32[]{:S(2)}) collective-permute-start(bf16[21,128,128]{2,1,0:T(8,128)(2,1)S(1)} %collective-permute-done.5.refs_11_.refs_16_), channel_id=1, source_target_pairs={{0,32},{8,104},{16,48},{24,120},{32,64},{40,8},{48,80},{56,24},{64... | collective-permute-start | bytes 2064392 | tf_op jit(solution)/shard_map/ppermute | solution.py:89
  25.5 39.4 %copy-start.3 = (bf16[21,128,128]{2,1,0:T(8,128)(2,1)}, bf16[21,128,128]{2,1,0:T(8,128)(2,1)S(1)}, u32[]{:S(2)}) copy-start(bf16[21,128,128]{2,1,0:T(8,128)(2,1)S(1)} %collective-permute-done.refs_6_.refs_11_) | copy-start | bytes 2064388
  25.5 23.0 %collective-permute-start.11 = (bf16[21,128,128]{2,1,0:T(8,128)(2,1)S(1)}, bf16[21,128,128]{2,1,0:T(8,128)(2,1)}, u32[]{:S(2)}, u32[]{:S(2)}) collective-permute-start(bf16[21,128,128]{2,1,0:T(8,128)(2,1)S(1)} %collective-permute-done.5.refs_11_.refs_16_), channel_id=1, source_target_pairs={{0,96},{8,40},{16,112},{24,56},{32,0},{40,72},{48,16},{56,88},{64,... | collective-permute-start | bytes 2064392 | tf_op jit(solution)/shard_map/ppermute | solution.py:89
  35.9 17.3 %collective-permute-start.13 = (bf16[21,128,128]{2,1,0:T(8,128)(2,1)}, bf16[21,128,128]{2,1,0:T(8,128)(2,1)}, u32[]{:S(2)}, u32[]{:S(2)}) collective-permute-start(bf16[21,128,128]{2,1,0:T(8,128)(2,1)} %collective-permute-done.7.refs_7_.refs_13_.refs_18_), channel_id=1, source_target_pairs={{0,16},{8,24},{16,0},{24,8},{32,48},{40,56},{48,32},{56,40},{64,80... | collective-permute-start | bytes 2064392 | tf_op jit(solution)/shard_map/ppermute | solution.py:89
  39.1 25.9 %copy-start.4 = (bf16[21,128,128]{2,1,0:T(8,128)(2,1)}, bf16[21,128,128]{2,1,0:T(8,128)(2,1)S(1)}, u32[]{:S(2)}) copy-start(bf16[21,128,128]{2,1,0:T(8,128)(2,1)S(1)} %collective-permute-done.2.refs_8_.refs_13_) | copy-start | bytes 2064388
  39.1 26.9 %collective-permute-start.6 = (bf16[21,128,128]{2,1,0:T(8,128)(2,1)S(1)}, bf16[21,128,128]{2,1,0:T(8,128)(2,1)}, u32[]{:S(2)}, u32[]{:S(2)}) collective-permute-start(bf16[21,128,128]{2,1,0:T(8,128)(2,1)S(1)} %collective-permute-done.5.refs_11_.refs_16_), channel_id=1, source_target_pairs={{0,8},{8,0},{16,24},{24,16},{32,40},{40,32},{48,56},{56,48},{64,72... | collective-permute-start | bytes 2064392 | tf_op jit(solution)/shard_map/ppermute | solution.py:89
  39.2 35.8 %collective-permute-start.8 = (bf16[21,128,128]{2,1,0:T(8,128)(2,1)}, bf16[21,128,128]{2,1,0:T(8,128)(2,1)}, u32[]{:S(2)}, u32[]{:S(2)}) collective-permute-start(bf16[21,128,128]{2,1,0:T(8,128)(2,1)} %collective-permute-done.7.refs_7_.refs_13_.refs_18_), channel_id=1, source_target_pairs={{0,8},{8,0},{16,24},{24,16},{32,40},{40,32},{48,56},{56,48},{64,72... | collective-permute-start | bytes 2064392 | tf_op jit(solution)/shard_map/ppermute | solution.py:89
  48.6 26.4 %collective-permute-start.10 = (bf16[21,128,128]{2,1,0:T(8,128)(2,1)}, bf16[21,128,128]{2,1,0:T(8,128)(2,1)}, u32[]{:S(2)}, u32[]{:S(2)}) collective-permute-start(bf16[21,128,128]{2,1,0:T(8,128)(2,1)} %collective-permute-done.9.refs_9_.refs_15_.refs_20_), channel_id=1, source_target_pairs={{0,8},{8,0},{16,24},{24,16},{32,40},{40,32},{48,56},{56,48},{64,72... | collective-permute-start | bytes 2064392 | tf_op jit(solution)/shard_map/ppermute | solution.py:89
  48.6 26.4 %collective-permute-start.12 = (bf16[21,128,128]{2,1,0:T(8,128)(2,1)}, bf16[21,128,128]{2,1,0:T(8,128)(2,1)}, u32[]{:S(2)}, u32[]{:S(2)}) collective-permute-start(bf16[21,128,128]{2,1,0:T(8,128)(2,1)} %collective-permute-done.11.refs_11_.refs_17_.refs_22_), channel_id=1, source_target_pairs={{0,8},{8,0},{16,24},{24,16},{32,40},{40,32},{48,56},{56,48},{64,72... | collective-permute-start | bytes 2064392 | tf_op jit(solution)/shard_map/ppermute | solution.py:89
  53.2 21.8 %collective-permute-start.14 = (bf16[21,128,128]{2,1,0:T(8,128)(2,1)}, bf16[21,128,128]{2,1,0:T(8,128)(2,1)}, u32[]{:S(2)}, u32[]{:S(2)}) collective-permute-start(bf16[21,128,128]{2,1,0:T(8,128)(2,1)} %collective-permute-done.13.refs_13_.refs_19_.refs_24_), channel_id=1, source_target_pairs={{0,8},{8,0},{16,24},{24,16},{32,40},{40,32},{48,56},{56,48},{64,72... | collective-permute-start | bytes 2064392 | tf_op jit(solution)/shard_map/ppermute | solution.py:89
  89.2 73.0 %collective-permute-start.24 = (bf16[4,21,128,128]{3,2,1,0:T(8,128)(2,1)}, bf16[4,21,128,128]{3,2,1,0:T(8,128)(2,1)}, u32[]{:S(2)}, u32[]{:S(2)}) collective-permute-start(bf16[4,21,128,128]{3,2,1,0:T(8,128)(2,1)} %get-tuple-element.49), channel_id=1, source_target_pairs={{0,8},{8,0},{16,24},{24,16},{32,40},{40,32},{48,56},{56,48},{64,72... | collective-permute-start | bytes 8257544 | tf_op jit(solution)/shard_map/ppermute | solution.py:89
  105.0 11.2 %collective-permute-start.32 = (f32[40,128]{1,0:T(8,128)}, f32[40,128]{1,0:T(8,128)S(1)}, u32[]{:S(2)}, u32[]{:S(2)}) collective-permute-start(f32[40,128]{1,0:T(8,128)} %get-tuple-element.54), channel_id=1, source_target_pairs={{0,64},{8,72},{16,80},{24,88},{32,96},{40,104},{48,112},{56,120},{... | collective-permute-start | bytes 61448 | tf_op jit(solution)/shard_map/ppermute | solution.py:89
  105.9 10.3 %collective-permute-start.33 = (f32[40,128]{1,0:T(8,128)}, f32[40,128]{1,0:T(8,128)S(1)}, u32[]{:S(2)}, u32[]{:S(2)}) collective-permute-start(f32[40,128]{1,0:T(8,128)} %get-tuple-element.54), channel_id=1, source_target_pairs={{0,96},{8,104},{16,112},{24,120},{32,64},{40,72},{48,80},{56,88},{... | collective-permute-start | bytes 61448 | tf_op jit(solution)/shard_map/ppermute | solution.py:89
  109.0 7.3 %collective-permute-start.31 = (f32[40,128]{1,0:T(8,128)}, f32[40,128]{1,0:T(8,128)S(1)}, u32[]{:S(2)}, u32[]{:S(2)}) collective-permute-start(f32[40,128]{1,0:T(8,128)} %get-tuple-element.54), channel_id=1, source_target_pairs={{0,32},{8,40},{16,48},{24,56},{32,0},{40,8},{48,16},{56,24},{64,96... | collective-permute-start | bytes 61448 | tf_op jit(solution)/shard_map/ppermute | solution.py:89
  116.1 62.6 %collective-permute-start.23 = (bf16[4,21,128,128]{3,2,1,0:T(8,128)(2,1)}, bf16[4,21,128,128]{3,2,1,0:T(8,128)(2,1)S(1)}, u32[]{:S(2)}, u32[]{:S(2)}) collective-permute-start(bf16[4,21,128,128]{3,2,1,0:T(8,128)(2,1)} %get-tuple-element.47), channel_id=1, source_target_pairs={{0,8},{8,0},{16,24},{24,16},{32,40},{40,32},{48,56},{56,48},{64,72... | collective-permute-start | bytes 8257544 | tf_op jit(solution)/shard_map/ppermute | solution.py:89
  116.3 5.4 %collective-permute-start.35 = (f32[40,128]{1,0:T(8,128)S(1)}, f32[40,128]{1,0:T(8,128)S(1)}, u32[]{:S(2)}, u32[]{:S(2)}) collective-permute-start(f32[40,128]{1,0:T(8,128)S(1)} %add_add_fusion.1), channel_id=1, source_target_pairs={{0,16},{8,24},{16,0},{24,8},{32,48},{40,56},{48,32},{56,40},{64,80... | collective-permute-start | bytes 61448 | tf_op jit(solution)/shard_map/ppermute | solution.py:89
  119.6 4.7 %collective-permute-start.36 = (f32[40,128]{1,0:T(8,128)S(1)}, f32[40,128]{1,0:T(8,128)S(1)}, u32[]{:S(2)}, u32[]{:S(2)}) collective-permute-start(f32[40,128]{1,0:T(8,128)S(1)} %add_add_fusion.1), channel_id=1, source_target_pairs={{0,24},{8,16},{16,8},{24,0},{32,56},{40,48},{48,40},{56,32},{64,88... | collective-permute-start | bytes 61448 | tf_op jit(solution)/shard_map/ppermute | solution.py:89
  119.7 4.5 %collective-permute-start.34 = (f32[40,128]{1,0:T(8,128)S(1)}, f32[40,128]{1,0:T(8,128)S(1)}, u32[]{:S(2)}, u32[]{:S(2)}) collective-permute-start(f32[40,128]{1,0:T(8,128)S(1)} %add_add_fusion.1), channel_id=1, source_target_pairs={{0,8},{8,0},{16,24},{24,16},{32,40},{40,32},{48,56},{56,48},{64,72... | collective-permute-start | bytes 61448 | tf_op jit(solution)/shard_map/ppermute | solution.py:89
  124.3 3.9 %collective-permute-start.37 = (f32[40,128]{1,0:T(8,128)S(1)}, f32[40,128]{1,0:T(8,128)S(1)}, u32[]{:S(2)}, u32[]{:S(2)}) collective-permute-start(f32[40,128]{1,0:T(8,128)S(1)} %add_add_fusion), channel_id=1, source_target_pairs={{0,2},{1,3},{2,0},{3,1},{4,6},{5,7},{6,4},{7,5},{8,10},{9,11},{10,... | collective-permute-start | bytes 61448 | tf_op jit(solution)/shard_map/ppermute | solution.py:93
  128.2 12.8 %copy-start.10 = (f32[192,128]{1,0:T(8,128)S(1)}, f32[192,128]{1,0:T(8,128)}, u32[]{:S(2)}) copy-start(f32[192,128]{1,0:T(8,128)} %get-tuple-element.40.refs_7_) | copy-start | bytes 294916
  128.2 11.9 %collective-permute-start.38 = (f32[40,128]{1,0:T(8,128)S(1)}, f32[40,128]{1,0:T(8,128)S(1)}, u32[]{:S(2)}, u32[]{:S(2)}) collective-permute-start(f32[40,128]{1,0:T(8,128)S(1)} %add.266), channel_id=1, source_target_pairs={{0,4},{1,5},{2,6},{3,7},{4,0},{5,1},{6,2},{7,3},{8,12},{9,13},{10,... | collective-permute-start | bytes 61448 | tf_op jit(solution)/shard_map/ppermute | solution.py:93
  139.4 22.6 %copy-start.8 = (bf16[2,208,512]{2,1,0:T(8,128)(2,1)S(1)}, bf16[2,208,512]{2,1,0:T(8,128)(2,1)}, u32[]{:S(2)}) copy-start(bf16[2,208,512]{2,1,0:T(8,128)(2,1)} %get-tuple-element.43) | copy-start | bytes 1277956
  139.4 13.6 %collective-permute-start.15 = (bf16[2,192,512]{2,1,0:T(8,128)(2,1)}, bf16[2,192,512]{2,1,0:T(8,128)(2,1)}, u32[]{:S(2)}, u32[]{:S(2)}) collective-permute-start(bf16[2,192,512]{2,1,0:T(8,128)(2,1)} %get-tuple-element.38), channel_id=1, source_target_pairs={{0,2},{1,3},{2,4},{3,5},{4,6},{5,7},{6,0},{7,1},{8,14},{9,15},{10,... | collective-permute-start | bytes 1179656 | tf_op jit(solution)/shard_map/ppermute | solution.py:93
  140.1 4.3 %collective-permute-start.39 = (f32[40,128]{1,0:T(8,128)S(1)}, f32[40,128]{1,0:T(8,128)S(1)}, u32[]{:S(2)}, u32[]{:S(2)}) collective-permute-start(f32[40,128]{1,0:T(8,128)S(1)} %add.267), channel_id=1, source_target_pairs={{0,1},{1,0},{2,3},{3,2},{4,5},{5,4},{6,7},{7,6},{8,9},{9,8},{10,11... | collective-permute-start | bytes 61448 | tf_op jit(solution)/shard_map/ppermute | solution.py:93
  141.8 29.4 %collective-permute-start.21 = (bf16[2,208,512]{2,1,0:T(8,128)(2,1)}, bf16[2,208,512]{2,1,0:T(8,128)(2,1)S(1)}, u32[]{:S(2)}, u32[]{:S(2)}) collective-permute-start(bf16[2,208,512]{2,1,0:T(8,128)(2,1)} %get-tuple-element.45), channel_id=1, source_target_pairs={{0,6},{1,7},{2,0},{3,1},{4,2},{5,3},{6,4},{7,5},{8,10},{9,11},{10,... | collective-permute-start | bytes 1277960 | tf_op jit(solution)/shard_map/ppermute | solution.py:93
  144.4 17.5 %collective-permute-start.19 = (bf16[2,208,512]{2,1,0:T(8,128)(2,1)}, bf16[2,208,512]{2,1,0:T(8,128)(2,1)S(1)}, u32[]{:S(2)}, u32[]{:S(2)}) collective-permute-start(bf16[2,208,512]{2,1,0:T(8,128)(2,1)} %get-tuple-element.44), channel_id=1, source_target_pairs={{0,2},{1,3},{2,4},{3,5},{4,6},{5,7},{6,0},{7,1},{8,14},{9,15},{10,... | collective-permute-start | bytes 1277960 | tf_op jit(solution)/shard_map/ppermute | solution.py:93
  153.0 16.1 %collective-permute-start.17 = (bf16[2,192,512]{2,1,0:T(8,128)(2,1)}, bf16[2,192,512]{2,1,0:T(8,128)(2,1)S(1)}, u32[]{:S(2)}, u32[]{:S(2)}) collective-permute-start(bf16[2,192,512]{2,1,0:T(8,128)(2,1)} %get-tuple-element.39), channel_id=1, source_target_pairs={{0,6},{1,7},{2,0},{3,1},{4,2},{5,3},{6,4},{7,5},{8,10},{9,11},{10,... | collective-permute-start | bytes 1179656 | tf_op jit(solution)/shard_map/ppermute | solution.py:93
  162.0 9.0 %collective-permute-start.16 = (bf16[2,192,512]{2,1,0:T(8,128)(2,1)S(1)}, bf16[2,192,512]{2,1,0:T(8,128)(2,1)S(1)}, u32[]{:S(2)}, u32[]{:S(2)}) collective-permute-start(bf16[2,192,512]{2,1,0:T(8,128)(2,1)S(1)} %add_convert_fusion.4), channel_id=1, source_target_pairs={{0,2},{1,3},{2,4},{3,5},{4,6},{5,7},{6,0},{7,1},{8,14},{9,15},{10,... | collective-permute-start | bytes 1179656 | tf_op jit(solution)/shard_map/ppermute | solution.py:93
  164.6 28.8 %collective-permute-start.28 = (bf16[2,21,128,128]{3,2,1,0:T(8,128)(2,1)S(1)}, bf16[2,21,128,128]{3,2,1,0:T(8,128)(2,1)S(1)}, u32[]{:S(2)}, u32[]{:S(2)}) collective-permute-start(bf16[2,21,128,128]{3,2,1,0:T(8,128)(2,1)S(1)} %add_convert_fusion), channel_id=1, source_target_pairs={{0,96},{8,40},{16,112},{24,56},{32,0},{40,72},{48,16},{56,88},{64,... | collective-permute-start | bytes 4128776 | tf_op jit(solution)/shard_map/ppermute | solution.py:89
  169.1 9.4 %collective-permute-start.20 = (bf16[2,208,512]{2,1,0:T(8,128)(2,1)S(1)}, bf16[2,208,512]{2,1,0:T(8,128)(2,1)S(1)}, u32[]{:S(2)}, u32[]{:S(2)}) collective-permute-start(bf16[2,208,512]{2,1,0:T(8,128)(2,1)S(1)} %add_convert_fusion.3), channel_id=1, source_target_pairs={{0,2},{1,3},{2,4},{3,5},{4,6},{5,7},{6,0},{7,1},{8,14},{9,15},{10,... | collective-permute-start | bytes 1277960 | tf_op jit(solution)/shard_map/ppermute | solution.py:93
  171.0 17.5 %collective-permute-start.25 = (bf16[21,128,128]{2,1,0:T(8,128)(2,1)S(1)}, bf16[21,128,128]{2,1,0:T(8,128)(2,1)S(1)}, u32[]{:S(2)}, u32[]{:S(2)}) collective-permute-start(bf16[21,128,128]{2,1,0:T(8,128)(2,1)S(1)} %get-tuple-element.60), channel_id=1, source_target_pairs={{0,16},{8,24},{16,0},{24,8},{32,48},{40,56},{48,32},{56,40},{64,80... | collective-permute-start | bytes 2064392 | tf_op jit(solution)/shard_map/ppermute | solution.py:89
  171.0 17.5 %copy-start.6 = (bf16[4,21,128,128]{3,2,1,0:T(8,128)(2,1)S(1)}, bf16[4,21,128,128]{3,2,1,0:T(8,128)(2,1)}, u32[]{:S(2)}) copy-start(bf16[4,21,128,128]{3,2,1,0:T(8,128)(2,1)} %get-tuple-element.50) | copy-start | bytes 8257540
  171.2 30.4 %collective-permute-start.18 = (bf16[192,512]{1,0:T(8,128)(2,1)S(1)}, bf16[192,512]{1,0:T(8,128)(2,1)S(1)}, u32[]{:S(2)}, u32[]{:S(2)}) collective-permute-start(bf16[192,512]{1,0:T(8,128)(2,1)S(1)} %fusion.16), channel_id=1, source_target_pairs={{0,1},{1,0},{2,3},{3,2},{4,5},{5,4},{6,7},{7,6},{8,9},{9,8},{10,11... | collective-permute-start | bytes 589832 | tf_op jit(solution)/shard_map/ppermute | solution.py:93
  178.7 14.7 %collective-permute-start.29 = (bf16[21,128,128]{2,1,0:T(8,128)(2,1)S(1)}, bf16[21,128,128]{2,1,0:T(8,128)(2,1)S(1)}, u32[]{:S(2)}, u32[]{:S(2)}) collective-permute-start(bf16[21,128,128]{2,1,0:T(8,128)(2,1)S(1)} %get-tuple-element.61), channel_id=1, source_target_pairs={{0,32},{8,104},{16,48},{24,120},{32,64},{40,8},{48,80},{56,24},{64... | collective-permute-start | bytes 2064392 | tf_op jit(solution)/shard_map/ppermute | solution.py:89
  188.8 12.2 %collective-permute-start.26 = (bf16[21,128,128]{2,1,0:T(8,128)(2,1)S(1)}, bf16[21,128,128]{2,1,0:T(8,128)(2,1)S(1)}, u32[]{:S(2)}, u32[]{:S(2)}) collective-permute-start(bf16[21,128,128]{2,1,0:T(8,128)(2,1)S(1)} %fusion.2), channel_id=1, source_target_pairs={{0,32},{8,104},{16,48},{24,120},{32,64},{40,8},{48,80},{56,24},{64... | collective-permute-start | bytes 2064392 | tf_op jit(solution)/shard_map/ppermute | solution.py:89
  190.2 11.3 %collective-permute-start.22 = (bf16[208,512]{1,0:T(8,128)(2,1)S(1)}, bf16[208,512]{1,0:T(8,128)(2,1)S(1)}, u32[]{:S(2)}, u32[]{:S(2)}) collective-permute-start(bf16[208,512]{1,0:T(8,128)(2,1)S(1)} %fusion.15), channel_id=1, source_target_pairs={{0,1},{1,0},{2,3},{3,2},{4,5},{5,4},{6,7},{7,6},{8,9},{9,8},{10,11... | collective-permute-start | bytes 638984 | tf_op jit(solution)/shard_map/ppermute | solution.py:93
  193.9 15.5 %collective-permute-start.30 = (bf16[21,128,128]{2,1,0:T(8,128)(2,1)S(1)}, bf16[21,128,128]{2,1,0:T(8,128)(2,1)S(1)}, u32[]{:S(2)}, u32[]{:S(2)}) collective-permute-start(bf16[21,128,128]{2,1,0:T(8,128)(2,1)S(1)} %fusion.1), channel_id=1, source_target_pairs={{0,16},{8,24},{16,0},{24,8},{32,48},{40,56},{48,32},{56,40},{64,80... | collective-permute-start | bytes 2064392 | tf_op jit(solution)/shard_map/ppermute | solution.py:89
  201.4 12.2 %collective-permute-start.27 = (bf16[21,128,128]{2,1,0:T(8,128)(2,1)S(1)}, bf16[21,128,128]{2,1,0:T(8,128)(2,1)S(1)}, u32[]{:S(2)}, u32[]{:S(2)}) collective-permute-start(bf16[21,128,128]{2,1,0:T(8,128)(2,1)S(1)} %fusion.3), channel_id=1, source_target_pairs={{0,32},{8,104},{16,48},{24,120},{32,64},{40,8},{48,80},{56,24},{64... | collective-permute-start | bytes 2064392 | tf_op jit(solution)/shard_map/ppermute | solution.py:89
  (9 other events, 85.8 us)
where the time goes:
time: 216 us; the launch traced here: 215 us
  waiting for transfers between devices  92 us (43%)
  Pallas kernels  66.2 us (31%)
  starting transfers between devices  41.5 us (19%)
  other arithmetic  11.6 us (5%)
  local copies, waits for them, and re-layouts  2.57 us (1%)
    ppermute x29, waiting for transfers between devices, over_dp(): return lax.ppermute(value, 'dp', dp_perm(kind))  67 us
    ppermute x29, starting transfers between devices, over_dp(): return lax.ppermute(value, 'dp', dp_perm(kind))  31 us
    ppermute x11, waiting for transfers between devices, over_tensor(): return lax.ppermute(value, ('dp', 'tensor'), tensor_perm(kind))  25 us
    pallas_call x1, Pallas kernels, input_call(): pl.pallas_call(functools.partial(input_kernel, share), out_shape=(piece,)...  14.8 us
    pallas_call x1, Pallas kernels, late_call(): pl.pallas_call(functools.partial(late_kernel, share, count), out_shape=(j...  14.2 us
    pallas_call x1, Pallas kernels, norm_call(): pl.pallas_call(norm_kernel, out_shape=(jax.ShapeDtypeStruct((tokens, widt...  11.7 us
    ppermute x11, starting transfers between devices, over_tensor(): return lax.ppermute(value, ('dp', 'tensor'), tensor_perm(kind))  10.5 us
    pallas_call x1, Pallas kernels, early_call(): pl.pallas_call(functools.partial(early_kernel, share, count), out_shape=(...  8.87 us
  transfers between devices with their start and end apart: 40, of which 17 were waited for; matrix products, arithmetic and copies ran while one was open for 6% of the time, Pallas kernels for 23%

commit v1 on v0

--- a/solution.py
+++ b/solution.py
@@ -18,18 +18,18 @@
 OWN, YY, A1, B1, A2, YA, YB, Y2 = range(8)
 AHEAD = (0, 0, -1, 1, 2, -1, 1, 2)
 TURN = (0, 1, 0, 0, 0, 1, 1, 1)
-EARLY = [(chip, flip) for chip in (OWN, A1, B1, YY) for flip in range(2)]
-LATE = [(chip, flip) for chip in (A2, YA, YB, Y2) for flip in range(2)]
+EARLY = [(chip, flip) for chip in (OWN, A1, B1, YY, A2) for flip in range(2)]
+LATE = [(chip, flip) for chip in (YA, YB, Y2) for flip in range(2)]
 FIRST = (Y2, YB, YA, A1)
 SECOND = (A2, B1, YY, OWN)
 FIRST_SLOTS = [(chip, flip) for chip in FIRST for flip in range(2)]
 SECOND_SLOTS = [(chip, flip) for chip in SECOND for flip in range(2)]
 TABLE = EARLY + LATE + FIRST_SLOTS + SECOND_SLOTS
-AT_EARLY, AT_LATE, AT_FIRST, AT_SECOND = 0, 8, 16, 24
+AT_EARLY, AT_LATE, AT_FIRST, AT_SECOND = 0, 10, 16, 24
 EXTRA = 16
-TILE = 16
+TILE = 64
 ROWS = 32
-VMEM_LIMIT = 60 * 1024 * 1024
+MIB = 1024 * 1024
 
 
 BF = jnp.bfloat16
@@ -119,31 +119,37 @@
 
 def norm_kernel(index, weights, h0, h1, h2, h3, grad_out, gain, normed, stats, kept):
     tile, width = normed.shape
-    size = 512
-    zero = jnp.zeros((tile, BS), F32)
-    squares, moments, cots = zero, [zero] * 4, [zero] * 4
-    for at in range(0, width, size):
-        cut = slice(at, at + size)
-        layers = [h[0, :, cut].astype(F32) for h in (h0, h1, h2, h3)]
-        mixed = weights[0] * layers[0]
-        for slot in range(1, 4):
-            mixed = mixed + weights[slot] * layers[slot]
-        kept[:, cut] = mixed
-        squares = squares + fold(mixed * mixed)
-        cot = grad_out[:, cut].astype(F32)
+    size, rows = 512, 16
+
+    def some_rows(step, carry):
+        here = pl.ds(pl.multiple_of(step * rows, rows), rows)
+        zero = jnp.zeros((rows, BS), F32)
+        squares, moments, cots = zero, [zero] * 4, [zero] * 4
+        for at in range(0, width, size):
+            cut = slice(at, at + size)
+            layers = [h[0, here, cut].astype(F32) for h in (h0, h1, h2, h3)]
+            mixed = weights[0] * layers[0]
+            for slot in range(1, 4):
+                mixed = mixed + weights[slot] * layers[slot]
+            kept[here, cut] = mixed
+            squares = squares + fold(mixed * mixed)
+            cot = grad_out[here, cut].astype(F32)
+            for slot in range(4):
+                moments[slot] = moments[slot] + fold(mixed * layers[slot])
+                cots[slot] = cots[slot] + fold(cot * layers[slot])
+        scale = lax.rsqrt(jnp.sum(squares, axis=-1, keepdims=True) / width + EPSILON)
+        for at in range(0, width, size):
+            cut = slice(at, at + size)
+            normed[here, cut] = (kept[here, cut] * scale * gain[:, cut]).astype(BF)
+        lane = lax.broadcasted_iota(jnp.int32, (rows, BS), 1)
+        found = jnp.where(lane == 0, scale, 0.0)
         for slot in range(4):
-            moments[slot] = moments[slot] + fold(mixed * layers[slot])
-            cots[slot] = cots[slot] + fold(cot * layers[slot])
-    scale = lax.rsqrt(jnp.sum(squares, axis=-1, keepdims=True) / width + EPSILON)
-    for at in range(0, width, size):
-        cut = slice(at, at + size)
-        normed[:, cut] = (kept[:, cut] * scale * gain[:, cut]).astype(BF)
-    lane = lax.broadcasted_iota(jnp.int32, stats.shape, 1)
-    found = jnp.where(lane == 0, scale, 0.0)
-    for slot in range(4):
-        found = jnp.where(lane == 1 + slot, jnp.sum(moments[slot], axis=-1, keepdims=True), found)
-        found = jnp.where(lane == 5 + slot, jnp.sum(cots[slot], axis=-1, keepdims=True), found)
-    stats[...] = found
+            found = jnp.where(lane == 1 + slot, jnp.sum(moments[slot], axis=-1, keepdims=True), found)
+            found = jnp.where(lane == 5 + slot, jnp.sum(cots[slot], axis=-1, keepdims=True), found)
+        stats[here] = found
+        return carry
+
+    lax.fori_loop(0, tile // rows, some_rows, 0)
 
 
 def norm_call(depth_index, depth_weights, history, grad_out, gain):
@@ -174,7 +180,7 @@
                 pl.BlockSpec((TILE, width), lambda i, index: (i, 0)),
             ],
         ),
-        compiler_params=pltpu.CompilerParams(vmem_limit_bytes=VMEM_LIMIT),
+        compiler_params=pltpu.CompilerParams(vmem_limit_bytes=24 * MIB),
         cost_estimate=pl.CostEstimate(flops=tokens * width * 30, bytes_accessed=tokens * width * 12, transcendentals=0),
         name="norm",
     )(depth_index, depth_weights, history, history, history, history, grad_out, gain.reshape(1, width))
@@ -307,7 +313,7 @@
             pltpu.VMEM((count * share, BS, BS), BF),
             pltpu.SemaphoreType.DMA((count, 3)),
         ],
-        compiler_params=pltpu.CompilerParams(vmem_limit_bytes=VMEM_LIMIT),
+        compiler_params=pltpu.CompilerParams(vmem_limit_bytes=18 * MIB),
         cost_estimate=pl.CostEstimate(flops=3 * 56 * 192 * 128 * 256, bytes_accessed=12_000_000, transcendentals=0),
         name="early",
     )(table, rows, cols, normed, grad_out, *shards)
@@ -366,7 +372,7 @@
             pltpu.SemaphoreType.DMA((count, 3)),
             pltpu.SemaphoreType.DMA((half, 2)),
         ],
-        compiler_params=pltpu.CompilerParams(vmem_limit_bytes=VMEM_LIMIT),
+        compiler_params=pltpu.CompilerParams(vmem_limit_bytes=34 * MIB),
         cost_estimate=pl.CostEstimate(flops=6 * 56 * 192 * 128 * 256, bytes_accessed=20_000_000, transcendentals=0),
         name="late",
     )(table, rows, cols, normed, grad_out, gate_up, back, *shards)
@@ -390,7 +396,7 @@
             pltpu.VMEM((half, 2, 3 * share, BS, BS), BF),
             pltpu.SemaphoreType.DMA((half, 2)),
         ],
-        compiler_params=pltpu.CompilerParams(vmem_limit_bytes=VMEM_LIMIT),
+        compiler_params=pltpu.CompilerParams(vmem_limit_bytes=16 * MIB),
         cost_estimate=pl.CostEstimate(flops=3 * 56 * 192 * 128 * 256, bytes_accessed=10_000_000, transcendentals=0),
         name="rest",
     )(table, rows, cols, normed, grad_out, hidden, pre)
@@ -494,7 +500,7 @@
             pltpu.SemaphoreType.DMA((N_DP, 2)),
             pltpu.SemaphoreType.DMA((4,)),
         ],
-        compiler_params=pltpu.CompilerParams(vmem_limit_bytes=VMEM_LIMIT),
+        compiler_params=pltpu.CompilerParams(vmem_limit_bytes=30 * MIB),
         cost_estimate=pl.CostEstimate(flops=2 * 112 * 192 * 128 * 256, bytes_accessed=20_000_000, transcendentals=0),
         name="input_grad",
     )(order, rows, cols, place, depth_index, depth_weights, pre, stats, gain.reshape(1, width), history, *shards)
@@ -540,30 +546,38 @@
             pltpu.VMEM((tokens, width), F32),
             pltpu.SemaphoreType.DMA((N_DP, 1)),
         ],
-        compiler_params=pltpu.CompilerParams(vmem_limit_bytes=VMEM_LIMIT),
+        compiler_params=pltpu.CompilerParams(vmem_limit_bytes=16 * MIB),
         cost_estimate=pl.CostEstimate(flops=112 * 192 * 128 * 256, bytes_accessed=10_000_000, transcendentals=0),
         name="output",
     )(order, rows, cols, place, hidden, *shards)
 
 
+def barrier(*values):
+    return lax.optimization_barrier(values)
+
+
 def add(*values):
     return sum(v.astype(F32) for v in values)
 
 
-def reduce_tensor(pieces):
+def reduce_tensor(pieces, after, last):
     own, to_a, to_b, far = pieces
     near = add(to_a, over_tensor(far, "a")).astype(BF)
-    total = add(own, over_tensor(near, "a"), over_tensor(to_b, "b"))
-    return add(total[0], over_tensor(total[1].astype(BF), "y"))
-
-
-def reduce_small(small):
-    for kinds in (("z1", "z2", "z3"), ("c", "y", "yc")):
-        one, two, three = [over_dp(small, kind) for kind in kinds]
-        small = (small + one) + (two + three)
-    for kind in ("1", "2", "y"):
-        small = small + over_tensor(small, kind)
-    return small
+    from_a, _ = barrier(over_tensor(near, "a"), after)
+    total = add(own, from_a, over_tensor(to_b, "b"))
+    moved, _ = barrier(over_tensor(total[1].astype(BF), "y"), last)
+    return add(total[0], moved)
+
+
+def reduce_small(small, after):
+    small = small + over_dp(small, "c")
+    small = small + over_dp(small, "y")
+    moved, _ = barrier(over_tensor(small, "y"), after)
+    small = small + moved
+    one, two, three = [over_dp(small, kind) for kind in ("z1", "z2", "z3")]
+    small = (small + one) + (two + three)
+    one, two, three = [over_tensor(small, kind) for kind in ("1", "2", "3")]
+    return (small + one) + (two + three)
 
 
 def per_device(
@@ -628,7 +642,6 @@
     far_y = over_dp(add(mine1[0], arrived1[0]).astype(BF), "y")
     across_a = over_dp(add(mine1[1], arrived1[1]).astype(BF), "a")
     both_b = over_dp(add(mine1[2:4], arrived1[2:4]).astype(BF), "b")
-    across_b, near_b = both_b[0], both_b[1]
 
     shards = [got[key] for key in EARLY + LATE]
     *back_pieces, small = input_call(
@@ -636,21 +649,24 @@
     )
     out_pieces = output_call(table, rows, cols, place, hidden, shards, share, width)
 
-    mine_y, arrived_y, across_a, across_b = lax.optimization_barrier((mine2, arrived2, across_a, across_b))
+    near_b = both_b[1]
+    mine_y, arrived_y, across_a, across_b = barrier(mine2, arrived2, across_a, both_b)
+    across_b = across_b[0]
     at = SECOND.index(YY)
     part[YY] = add(mine_y[at], arrived_y[at])
     far = add(part[A2], far_y).astype(BF)
     near = add(part[B1], over_dp(far, "a")).astype(BF)
-    across = over_dp(add(part[YY], across_a, across_b).astype(BF), "y")
+    across_low = add(part[YY], across_a, across_b).astype(BF)
+    across = over_dp(across_low, "y")
     near_a = over_dp(near, "a")
     own1, own2 = mine2[SECOND.index(OWN)], arrived2[SECOND.index(OWN)]
     block_grads = [
         add(*[v[k * share : (k + 1) * share] for v in (own1, own2, near_a, near_b, across)]) for k in range(3)
     ]
 
-    back = reduce_tensor(back_pieces)
-    ffn = reduce_tensor(out_pieces)
-    small = reduce_small(small)
+    back = reduce_tensor(back_pieces, near, block_grads[0])
+    ffn = reduce_tensor(out_pieces, near, block_grads[0])
+    small = reduce_small(small, across_low)
 
     mixed = lax.dynamic_slice_in_dim(kept, share_start, share_width, 1)
     layer_out = (mixed + ffn).astype(BF)

time: 216 us -> 207 us (0.958)
  waiting for transfers between devices: 92 us -> 66.3 us
  local copies, waits for them, and re-layouts: 2.57 us -> 24.9 us
  Pallas kernels: 66.2 us -> 54.9 us
  starting transfers between devices: 41.5 us -> 44.2 us
  other arithmetic: 11.6 us -> 13.9 us
    unnamed x34 -> x88, local copies, waits for them, and re-layouts: 0.08 us -> 23.7 us
    ppermute x29 -> x28, waiting for transfers between devices: 67 us -> 49.3 us  [over_dp(): return lax.ppermute(value, 'dp', dp_perm(kind))]
    ppermute x11 -> x12, waiting for transfers between devices: 25 us -> 17 us  [over_tensor(): return lax.ppermute(value, ('dp', 'tensor'), tensor_perm(kind))]
    pallas_call x1, Pallas kernels: 11.7 us -> 5.34 us  [norm_call(): pl.pallas_call(norm_kernel, out_shape=(jax.ShapeDtypeStruct((tokens, widt...]
    ppermute x29 -> x28, starting transfers between devices: 31 us -> 33.8 us  [over_dp(): return lax.ppermute(value, 'dp', dp_perm(kind))]
    pallas_call x1, Pallas kernels: 14.2 us -> 11.4 us  [late_call(): pl.pallas_call(functools.partial(late_kernel, share, count), out_shape=(j...]
    ppermute x11 -> x12, starting transfers between devices: 10.5 us -> 10.4 us  [over_tensor(): return lax.ppermute(value, ('dp', 'tensor'), tensor_perm(kind))]
  transfers between devices with their start and end apart: 40 -> 40, of which waited for: 17 -> 15; matrix products, arithmetic and copies ran while one was open for 6% -> 6% of each run, Pallas kernels for 23% -> 20%
where the time goes in v1:
time: 207 us; the launch traced here: 205 us
  waiting for transfers between devices  66.3 us (32%)
  Pallas kernels  54.9 us (27%)
  starting transfers between devices  44.2 us (21%)
  local copies, waits for them, and re-layouts  24.9 us (12%)
  other arithmetic  13.9 us (7%)
    ppermute x28, waiting for transfers between devices, over_dp(): return lax.ppermute(value, 'dp', dp_perm(kind))  49.3 us
    ppermute x28, starting transfers between devices, over_dp(): return lax.ppermute(value, 'dp', dp_perm(kind))  33.8 us
    unnamed x88, local copies, waits for them, and re-layouts  23.7 us
    ppermute x12, waiting for transfers between devices, over_tensor(): return lax.ppermute(value, ('dp', 'tensor'), tensor_perm(kind))  17 us
    pallas_call x1, Pallas kernels, input_call(): pl.pallas_call(functools.partial(input_kernel, share), out_shape=(piece,)...  13 us
    pallas_call x1, Pallas kernels, late_call(): pl.pallas_call(functools.partial(late_kernel, share, count), out_shape=(j...  11.4 us
    ppermute x12, starting transfers between devices, over_tensor(): return lax.ppermute(value, ('dp', 'tensor'), tensor_perm(kind))  10.4 us
    pallas_call x1, Pallas kernels, output_call(): pl.pallas_call(functools.partial(output_kernel, share), out_shape=(piece,...  8.85 us
  transfers between devices with their start and end apart: 40, of which 15 were waited for; matrix products, arithmetic and copies ran while one was open for 6% of the time, Pallas kernels for 20%

profile of v1, /device:TPU:0, one launch (start us, length us, event | category | flops | bytes accessed | tf_op | source)
XLA Modules:
  0.0 205.5 jit_solution(2449147771148585995)
XLA Ops:
  0.7 2.1 %join.1.refs_5_.refs_10_ = bf16[21,128,128]{2,1,0:T(8,128)(2,1)} custom-call(bf16[7,128,128]{2,1,0:T(8,128)(2,1)} %gate.1, bf16[7,128,128]{2,1,0:T(8,128)(2,1)} %up.1, bf16[7,128,128]{2,1,0:T(8,128)(2,1)} %down.1), custom_call_target="tpu_custom_call" | custom-call | tf_op jit(solution)/shard_map/join/pallas_call | solution.py:202
  2.8 2.1 %collective-permute-start.1 = (bf16[21,128,128]{2,1,0:T(8,128)(2,1)}, bf16[21,128,128]{2,1,0:T(8,128)(2,1)}, u32[]{:S(2)}, u32[]{:S(2)}) collective-permute-start(bf16[21,128,128]{2,1,0:T(8,128)(2,1)} %join.1.refs_5_.refs_10_), channel_id=1, source_target_pairs={{0,32},{8,104},{16,48},{24,120},{32,64},{40,8},{48,80},{56,24},{64... | collective-permute-start | bytes 2064392 | tf_op jit(solution)/shard_map/ppermute | solution.py:89
  4.9 3.2 %collective-permute-start.5 = (bf16[21,128,128]{2,1,0:T(8,128)(2,1)}, bf16[21,128,128]{2,1,0:T(8,128)(2,1)S(1)}, u32[]{:S(2)}, u32[]{:S(2)}) collective-permute-start(bf16[21,128,128]{2,1,0:T(8,128)(2,1)} %join.1.refs_5_.refs_10_), channel_id=1, source_target_pairs={{0,16},{8,24},{16,0},{24,8},{32,48},{40,56},{48,32},{56,40},{64,80... | collective-permute-start | bytes 2064392 | tf_op jit(solution)/shard_map/ppermute | solution.py:89
  8.1 2.2 %collective-permute-start.3 = (bf16[21,128,128]{2,1,0:T(8,128)(2,1)}, bf16[21,128,128]{2,1,0:T(8,128)(2,1)S(1)}, u32[]{:S(2)}, u32[]{:S(2)}) collective-permute-start(bf16[21,128,128]{2,1,0:T(8,128)(2,1)} %join.1.refs_5_.refs_10_), channel_id=1, source_target_pairs={{0,96},{8,40},{16,112},{24,56},{32,0},{40,72},{48,16},{56,88},{64,... | collective-permute-start | bytes 2064392 | tf_op jit(solution)/shard_map/ppermute | solution.py:89
  10.3 8.6 %collective-permute-done.1.refs_7_.refs_12_ = bf16[21,128,128]{2,1,0:T(8,128)(2,1)} collective-permute-done((bf16[21,128,128]{2,1,0:T(8,128)(2,1)}, bf16[21,128,128]{2,1,0:T(8,128)(2,1)}, u32[]{:S(2)}, u32[]{:S(2)}) %collective-permute-start.1) | collective-permute-done | bytes 688160 | tf_op jit(solution)/shard_map/ppermute | solution.py:89
  18.9 2.2 %collective-permute-start.7 = (bf16[21,128,128]{2,1,0:T(8,128)(2,1)}, bf16[21,128,128]{2,1,0:T(8,128)(2,1)}, u32[]{:S(2)}, u32[]{:S(2)}) collective-permute-start(bf16[21,128,128]{2,1,0:T(8,128)(2,1)} %collective-permute-done.1.refs_7_.refs_12_), channel_id=1, source_target_pairs={{0,32},{8,104},{16,48},{24,120},{32,64},{40,8},{48,80},{56,24},{64... | collective-permute-start | bytes 2064392 | tf_op jit(solution)/shard_map/ppermute | solution.py:89
  21.1 3.1 %collective-permute-done.5.refs_11_.refs_16_ = bf16[21,128,128]{2,1,0:T(8,128)(2,1)S(1)} collective-permute-done((bf16[21,128,128]{2,1,0:T(8,128)(2,1)}, bf16[21,128,128]{2,1,0:T(8,128)(2,1)S(1)}, u32[]{:S(2)}, u32[]{:S(2)}) %collective-permute-start.5) | collective-permute-done | bytes 688160 | tf_op jit(solution)/shard_map/ppermute | solution.py:89
  24.2 1.8 collective-permute-start.11
  30.0 7.2 %collective-permute-done.7.refs_13_.refs_18_ = bf16[21,128,128]{2,1,0:T(8,128)(2,1)} collective-permute-done((bf16[21,128,128]{2,1,0:T(8,128)(2,1)}, bf16[21,128,128]{2,1,0:T(8,128)(2,1)}, u32[]{:S(2)}, u32[]{:S(2)}) %collective-permute-start.7) | collective-permute-done | bytes 688160 | tf_op jit(solution)/shard_map/ppermute | solution.py:89
  37.3 5.7 %collective-permute-start.13 = (bf16[21,128,128]{2,1,0:T(8,128)(2,1)}, bf16[21,128,128]{2,1,0:T(8,128)(2,1)}, u32[]{:S(2)}, u32[]{:S(2)}) collective-permute-start(bf16[21,128,128]{2,1,0:T(8,128)(2,1)} %collective-permute-done.7.refs_13_.refs_18_), channel_id=1, source_target_pairs={{0,16},{8,24},{16,0},{24,8},{32,48},{40,56},{48,32},{56,40},{64,80... | collective-permute-start | bytes 2064392 | tf_op jit(solution)/shard_map/ppermute | solution.py:89
  43.5 4.2 %collective-permute-done.9.refs_7_.refs_15_.refs_20_ = bf16[21,128,128]{2,1,0:T(8,128)(2,1)} collective-permute-done((bf16[21,128,128]{2,1,0:T(8,128)(2,1)S(1)}, bf16[21,128,128]{2,1,0:T(8,128)(2,1)}, u32[]{:S(2)}, u32[]{:S(2)}) %collective-permute-start.9) | collective-permute-done | bytes 688160 | tf_op jit(solution)/shard_map/ppermute | solution.py:89
  49.9 6.0 %collective-permute-done.13.refs_11_.refs_19_.refs_24_ = bf16[21,128,128]{2,1,0:T(8,128)(2,1)} collective-permute-done((bf16[21,128,128]{2,1,0:T(8,128)(2,1)}, bf16[21,128,128]{2,1,0:T(8,128)(2,1)}, u32[]{:S(2)}, u32[]{:S(2)}) %collective-permute-start.13) | collective-permute-done | bytes 688160 | tf_op jit(solution)/shard_map/ppermute | solution.py:89
  55.9 2.8 %copy-done = bf16[4,192,4096]{2,1,0:T(8,128)(2,1)S(1)} copy-done((bf16[4,192,4096]{2,1,0:T(8,128)(2,1)S(1)}, bf16[4,192,4096]{2,1,0:T(8,128)(2,1)}, u32[]{:S(2)}) %copy-start) | copy-done | bytes 6291480
  58.7 1.4 copy-done.2
  60.2 5.3 %norm.1 = (bf16[192,4096]{1,0:T(8,128)(2,1)S(1)}, f32[192,128]{1,0:T(8,128)S(1)}, f32[192,4096]{1,0:T(8,128)S(1)}) custom-call(s32[4]{0:T(128)S(1)} %copy-done.34, f32[4]{0:T(128)S(1)} %copy-done.35, bf16[4,192,4096]{2,1,0:T(8,128)(2,1)S(1)} %copy-done, bf16[4,192,4096]{2,1,0:T(8,128)(2,1)S(1)} %copy-done, bf16[4,192,4096]{2,1,0:T(8,128)(2,1)S(1)} %copy-done, ...), custom_call_target="tpu_custom_call" | custom-call | flops 23592960 | bytes 9437184 | tf_op jit(solution)/shard_map/norm/pallas_call | solution.py:161
  65.6 1.6 copy-done.33
  67.3 7.8 %early.1 = (f32[14,192,256]{2,1,0:T(8,128)S(1)}, f32[14,192,128]{2,1,0:T(8,128)S(1)}) custom-call(s32[32]{0:T(128)S(1)} %fusion.21.refs_0_.table, s32[112]{0:T(128)S(1)} %get-tuple-element.75.refs_1_.rows, s32[112]{0:T(128)S(1)} %get-tuple-element.74.refs_2_.cols, bf16[192,4096]{1,0:T(8,128)(2,1)S(1)} %get-tuple-element.37.refs_3_.normed, ...), custom_call_target="tpu_custom_call" | custom-call | flops 1056964608 | bytes 12000000 | tf_op jit(solution)/shard_map/early/pallas_call | solution.py:303
  75.2 11.4 %late.1 = (bf16[14,192,128]{2,1,0:T(8,128)(2,1)S(1)}, bf16[14,192,256]{2,1,0:T(8,128)(2,1)S(1)}, bf16[4,21,128,128]{3,2,1,0:T(8,128)(2,1)S(1)}, bf16[4,21,128,128]{3,2,1,0:T(8,128)(2,1)S(1)}) custom-call(s32[32]{0:T(128)S(1)} %fusion.21.refs_0_.table, s32[112]{0:T(128)S(1)} %get-tuple-element.75.refs_1_.rows, s32[112]{0:T(128)S(1)} %get-tuple-element.74.refs_2_.cols, ...), custom_call_target="tpu_custom_call" | custom-call | flops 2113929216 | bytes 20000000 | tf_op jit(solution)/shard_map/late/pallas_call | solution.py:356
  87.2 6.3 %rest.1 = (bf16[4,21,128,128]{3,2,1,0:T(8,128)(2,1)S(1)}, bf16[4,21,128,128]{3,2,1,0:T(8,128)(2,1)}) custom-call(s32[32]{0:T(128)S(1)} %fusion.21.refs_0_.table, s32[112]{0:T(128)S(1)} %get-tuple-element.75.refs_1_.rows, s32[112]{0:T(128)S(1)} %get-tuple-element.74.refs_2_.cols, bf16[192,4096]{1,0:T(8,128)(2,1)S(1)} %get-tuple-element.37.refs_3_.normed, ...), custom_call_target="tpu_custom_call" | custom-call | flops 1056964608 | bytes 10000000 | tf_op jit(solution)/shard_map/rest/pallas_call | solution.py:390
  93.6 1.6 copy-done.22
  95.2 1.6 fusion.4
  96.8 3.2 %collective-permute-start.19 = (bf16[21,128,128]{2,1,0:T(8,128)(2,1)}, bf16[21,128,128]{2,1,0:T(8,128)(2,1)}, u32[]{:S(2)}, u32[]{:S(2)}) collective-permute-start(bf16[21,128,128]{2,1,0:T(8,128)(2,1)} %get-tuple-element.71), channel_id=1, source_target_pairs={{0,16},{8,24},{16,0},{24,8},{32,48},{40,56},{48,32},{56,40},{64,80... | collective-permute-start | bytes 2064392 | tf_op jit(solution)/shard_map/ppermute | solution.py:89
  100.0 1.6 add_convert_fusion
  101.6 3.6 %collective-permute-start.24 = (bf16[2,21,128,128]{3,2,1,0:T(8,128)(2,1)}, bf16[2,21,128,128]{3,2,1,0:T(8,128)(2,1)}, u32[]{:S(2)}, u32[]{:S(2)}) collective-permute-start(bf16[2,21,128,128]{3,2,1,0:T(8,128)(2,1)} %add_convert_fusion), channel_id=1, source_target_pairs={{0,96},{8,40},{16,112},{24,56},{32,0},{40,72},{48,16},{56,88},{64,... | collective-permute-start | bytes 4128776 | tf_op jit(solution)/shard_map/ppermute | solution.py:89
  105.2 2.8 %copy-done.1 = bf16[4,192,4096]{2,1,0:T(8,128)(2,1)S(1)} copy-done((bf16[4,192,4096]{2,1,0:T(8,128)(2,1)S(1)}, bf16[4,192,4096]{2,1,0:T(8,128)(2,1)}, u32[]{:S(2)}) %copy-start.1) | copy-done | bytes 6291480
  113.5 1.3 copy-done.21
  114.8 13.0 %input_grad.1 = (bf16[2,208,512]{2,1,0:T(8,128)(2,1)S(1)}, bf16[2,208,512]{2,1,0:T(8,128)(2,1)S(1)}, bf16[2,208,512]{2,1,0:T(8,128)(2,1)S(1)}, bf16[2,208,512]{2,1,0:T(8,128)(2,1)S(1)}, f32[40,128]{1,0:T(8,128)S(1)}) custom-call(s32[32]{0:T(128)S(1)} %fusion.21.refs_0_.table, s32[112]{0:T(128)S(1)} %get-tuple-element.75.refs_1_.rows, ...), custom_call_target="tpu_custom_call" | custom-call | flops 1409286144 | bytes 20000000 | tf_op jit(solution)/shard_map/input_grad/pallas_call | solution.py:490
  128.0 8.8 %output.1 = (bf16[2,192,512]{2,1,0:T(8,128)(2,1)S(1)}, bf16[2,192,512]{2,1,0:T(8,128)(2,1)S(1)}, bf16[2,192,512]{2,1,0:T(8,128)(2,1)S(1)}, bf16[2,192,512]{2,1,0:T(8,128)(2,1)}) custom-call(s32[32]{0:T(128)S(1)} %fusion.21.refs_0_.table, s32[112]{0:T(128)S(1)} %get-tuple-element.75.refs_1_.rows, s32[112]{0:T(128)S(1)} %get-tuple-element.74.refs_2_.cols, ...), custom_call_target="tpu_custom_call" | custom-call | flops 704643072 | bytes 10000000 | tf_op jit(solution)/shard_map/output/pallas_call | solution.py:539
  139.2 1.5 collective-permute-start.15
  141.3 4.8 %collective-permute-done.32 = f32[40,128]{1,0:T(8,128)S(1)} collective-permute-done((f32[40,128]{1,0:T(8,128)S(1)}, f32[40,128]{1,0:T(8,128)S(1)}, u32[]{:S(2)}, u32[]{:S(2)}) %collective-permute-start.32) | collective-permute-done | bytes 20512 | tf_op jit(solution)/shard_map/ppermute | solution.py:89
  146.1 1.7 collective-permute-start.21
  148.2 2.0 fusion.1
  150.2 1.6 collective-permute-start.20
  151.9 7.2 %collective-permute-done.27 = bf16[2,208,512]{2,1,0:T(8,128)(2,1)S(1)} collective-permute-done((bf16[2,208,512]{2,1,0:T(8,128)(2,1)}, bf16[2,208,512]{2,1,0:T(8,128)(2,1)S(1)}, u32[]{:S(2)}, u32[]{:S(2)}) %collective-permute-start.27) | collective-permute-done | bytes 426016 | tf_op jit(solution)/shard_map/ppermute | solution.py:93
  159.2 1.3 collective-permute-done.25
  160.5 1.4 collective-permute-start.16
  163.2 1.7 fusion
  165.0 3.0 %collective-permute-done.20 = bf16[21,128,128]{2,1,0:T(8,128)(2,1)S(1)} collective-permute-done((bf16[21,128,128]{2,1,0:T(8,128)(2,1)S(1)}, bf16[21,128,128]{2,1,0:T(8,128)(2,1)S(1)}, u32[]{:S(2)}, u32[]{:S(2)}) %collective-permute-start.20) | collective-permute-done | bytes 688160 | tf_op jit(solution)/shard_map/ppermute | solution.py:89
  167.9 1.4 fusion.2
  169.4 6.5 %collective-permute-done.28 = bf16[2,208,512]{2,1,0:T(8,128)(2,1)S(1)} collective-permute-done((bf16[2,208,512]{2,1,0:T(8,128)(2,1)S(1)}, bf16[2,208,512]{2,1,0:T(8,128)(2,1)S(1)}, u32[]{:S(2)}, u32[]{:S(2)}) %collective-permute-start.28) | collective-permute-done | bytes 426016 | tf_op jit(solution)/shard_map/ppermute | solution.py:93
  175.9 3.3 %collective-permute-start.36 = (f32[40,128]{1,0:T(8,128)S(1)}, f32[40,128]{1,0:T(8,128)S(1)}, u32[]{:S(2)}, u32[]{:S(2)}) collective-permute-start(f32[40,128]{1,0:T(8,128)S(1)} %add.262), channel_id=1, source_target_pairs={{0,96},{8,104},{16,112},{24,120},{32,64},{40,72},{48,80},{56,88},{... | collective-permute-start | bytes 61448 | tf_op jit(solution)/shard_map/ppermute | solution.py:89
  180.9 7.8 %collective-permute-done.36 = f32[40,128]{1,0:T(8,128)S(1)} collective-permute-done((f32[40,128]{1,0:T(8,128)S(1)}, f32[40,128]{1,0:T(8,128)S(1)}, u32[]{:S(2)}, u32[]{:S(2)}) %collective-permute-start.36) | collective-permute-done | bytes 20512 | tf_op jit(solution)/shard_map/ppermute | solution.py:89
  188.7 1.8 collective-permute-start.39
  190.5 2.3 %collective-permute-start.37 = (f32[40,128]{1,0:T(8,128)S(1)}, f32[40,128]{1,0:T(8,128)S(1)}, u32[]{:S(2)}, u32[]{:S(2)}) collective-permute-start(f32[40,128]{1,0:T(8,128)S(1)} %add_add_fusion.1), channel_id=1, source_target_pairs={{0,2},{1,3},{2,0},{3,1},{4,6},{5,7},{6,4},{7,5},{8,10},{9,11},{10,... | collective-permute-start | bytes 61448 | tf_op jit(solution)/shard_map/ppermute | solution.py:93
  193.8 2.0 collective-permute-done.38
  196.9 3.3 %collective-permute-done.26 = bf16[21,128,128]{2,1,0:T(8,128)(2,1)S(1)} collective-permute-done((bf16[21,128,128]{2,1,0:T(8,128)(2,1)S(1)}, bf16[21,128,128]{2,1,0:T(8,128)(2,1)S(1)}, u32[]{:S(2)}, u32[]{:S(2)}) %collective-permute-start.26) | collective-permute-done | bytes 688160 | tf_op jit(solution)/shard_map/ppermute | solution.py:89
  200.2 2.8 %fusion.5 = (f32[7,128,128]{2,1,0:T(8,128)}, f32[7,128,128]{2,1,0:T(8,128)}, f32[7,128,128]{2,1,0:T(8,128)}) fusion(bf16[21,128,128]{2,1,0:T(8,128)(2,1)S(1)} %collective-permute-done.26, bf16[2,21,128,128]{3,2,1,0:T(8,128)(2,1)} %collective-permute-done.24, bf16[21,128,128]{2,1,0:T(8,128)(2,1)S(1)} %collective-permute-done.23, ...), kind=kLoop, calls=%fused_computation.17 | loop fusion | flops 3096576 | bytes 4816896 | tf_op jit(solution)/shard_map/add | solution.py:560
  203.5 2.0 fusion.10
  (154 shorter events, 22.0 us)
Async XLA Ops:
  0.6 55.3 %copy-start.32 = (f32[4096]{0:T(1024)S(1)}, f32[4096]{0:T(1024)}, u32[]{:S(2)}) copy-start(f32[4096]{0:T(1024)} %param.15) | copy-start | bytes 49156
  0.6 55.3 %copy-start.34 = (s32[4]{0:T(128)S(1)}, s32[4]{0:T(128)}, u32[]{:S(2)}) copy-start(s32[4]{0:T(128)} %refs_4_.5) | copy-start | bytes 52
  0.7 55.3 %copy-start.35 = (f32[4]{0:T(128)S(1)}, f32[4]{0:T(128)}, u32[]{:S(2)}) copy-start(f32[4]{0:T(128)} %refs_5_.1) | copy-start | bytes 52
  2.8 16.1 %collective-permute-start.1 = (bf16[21,128,128]{2,1,0:T(8,128)(2,1)}, bf16[21,128,128]{2,1,0:T(8,128)(2,1)}, u32[]{:S(2)}, u32[]{:S(2)}) collective-permute-start(bf16[21,128,128]{2,1,0:T(8,128)(2,1)} %join.1.refs_5_.refs_10_), channel_id=1, source_target_pairs={{0,32},{8,104},{16,48},{24,120},{32,64},{40,8},{48,80},{56,24},{64... | collective-permute-start | bytes 2064392 | tf_op jit(solution)/shard_map/ppermute | solution.py:89
  4.9 19.3 %collective-permute-start.5 = (bf16[21,128,128]{2,1,0:T(8,128)(2,1)}, bf16[21,128,128]{2,1,0:T(8,128)(2,1)S(1)}, u32[]{:S(2)}, u32[]{:S(2)}) collective-permute-start(bf16[21,128,128]{2,1,0:T(8,128)(2,1)} %join.1.refs_5_.refs_10_), channel_id=1, source_target_pairs={{0,16},{8,24},{16,0},{24,8},{32,48},{40,56},{48,32},{56,40},{64,80... | collective-permute-start | bytes 2064392 | tf_op jit(solution)/shard_map/ppermute | solution.py:89
  8.1 18.1 %collective-permute-start.3 = (bf16[21,128,128]{2,1,0:T(8,128)(2,1)}, bf16[21,128,128]{2,1,0:T(8,128)(2,1)S(1)}, u32[]{:S(2)}, u32[]{:S(2)}) collective-permute-start(bf16[21,128,128]{2,1,0:T(8,128)(2,1)} %join.1.refs_5_.refs_10_), channel_id=1, source_target_pairs={{0,96},{8,40},{16,112},{24,56},{32,0},{40,72},{48,16},{56,88},{64,... | collective-permute-start | bytes 2064392 | tf_op jit(solution)/shard_map/ppermute | solution.py:89
  10.3 18.0 %collective-permute-start = (bf16[21,128,128]{2,1,0:T(8,128)(2,1)}, bf16[21,128,128]{2,1,0:T(8,128)(2,1)S(1)}, u32[]{:S(2)}, u32[]{:S(2)}) collective-permute-start(bf16[21,128,128]{2,1,0:T(8,128)(2,1)} %join.1.refs_5_.refs_10_), channel_id=1, source_target_pairs={{0,8},{8,0},{16,24},{24,16},{32,40},{40,32},{48,56},{56,48},{64,72... | collective-permute-start | bytes 2064392 | tf_op jit(solution)/shard_map/ppermute | solution.py:89
  18.9 18.4 %collective-permute-start.7 = (bf16[21,128,128]{2,1,0:T(8,128)(2,1)}, bf16[21,128,128]{2,1,0:T(8,128)(2,1)}, u32[]{:S(2)}, u32[]{:S(2)}) collective-permute-start(bf16[21,128,128]{2,1,0:T(8,128)(2,1)} %collective-permute-done.1.refs_7_.refs_12_), channel_id=1, source_target_pairs={{0,32},{8,104},{16,48},{24,120},{32,64},{40,8},{48,80},{56,24},{64... | collective-permute-start | bytes 2064392 | tf_op jit(solution)/shard_map/ppermute | solution.py:89
  24.2 18.8 %collective-permute-start.11 = (bf16[21,128,128]{2,1,0:T(8,128)(2,1)S(1)}, bf16[21,128,128]{2,1,0:T(8,128)(2,1)S(1)}, u32[]{:S(2)}, u32[]{:S(2)}) collective-permute-start(bf16[21,128,128]{2,1,0:T(8,128)(2,1)S(1)} %collective-permute-done.5.refs_11_.refs_16_), channel_id=1, source_target_pairs={{0,96},{8,40},{16,112},{24,56},{32,0},{40,72},{48,16},{56,88},{64,... | collective-permute-start | bytes 2064392 | tf_op jit(solution)/shard_map/ppermute | solution.py:89
  26.0 21.7 %collective-permute-start.9 = (bf16[21,128,128]{2,1,0:T(8,128)(2,1)S(1)}, bf16[21,128,128]{2,1,0:T(8,128)(2,1)}, u32[]{:S(2)}, u32[]{:S(2)}) collective-permute-start(bf16[21,128,128]{2,1,0:T(8,128)(2,1)S(1)} %collective-permute-done.5.refs_11_.refs_16_), channel_id=1, source_target_pairs={{0,32},{8,104},{16,48},{24,120},{32,64},{40,8},{48,80},{56,24},{64... | collective-permute-start | bytes 2064392 | tf_op jit(solution)/shard_map/ppermute | solution.py:89
  26.2 21.5 %collective-permute-start.6 = (bf16[21,128,128]{2,1,0:T(8,128)(2,1)S(1)}, bf16[21,128,128]{2,1,0:T(8,128)(2,1)S(1)}, u32[]{:S(2)}, u32[]{:S(2)}) collective-permute-start(bf16[21,128,128]{2,1,0:T(8,128)(2,1)S(1)} %collective-permute-done.5.refs_11_.refs_16_), channel_id=1, source_target_pairs={{0,8},{8,0},{16,24},{24,16},{32,40},{40,32},{48,56},{56,48},{64,72... | collective-permute-start | bytes 2064392 | tf_op jit(solution)/shard_map/ppermute | solution.py:89
  29.2 19.9 %collective-permute-start.4 = (bf16[21,128,128]{2,1,0:T(8,128)(2,1)S(1)}, bf16[21,128,128]{2,1,0:T(8,128)(2,1)S(1)}, u32[]{:S(2)}, u32[]{:S(2)}) collective-permute-start(bf16[21,128,128]{2,1,0:T(8,128)(2,1)S(1)} %collective-permute-done.3.refs_9_.refs_14_), channel_id=1, source_target_pairs={{0,8},{8,0},{16,24},{24,16},{32,40},{40,32},{48,56},{56,48},{64,72... | collective-permute-start | bytes 2064392 | tf_op jit(solution)/shard_map/ppermute | solution.py:89
  37.3 18.6 %collective-permute-start.13 = (bf16[21,128,128]{2,1,0:T(8,128)(2,1)}, bf16[21,128,128]{2,1,0:T(8,128)(2,1)}, u32[]{:S(2)}, u32[]{:S(2)}) collective-permute-start(bf16[21,128,128]{2,1,0:T(8,128)(2,1)} %collective-permute-done.7.refs_13_.refs_18_), channel_id=1, source_target_pairs={{0,16},{8,24},{16,0},{24,8},{32,48},{40,56},{48,32},{56,40},{64,80... | collective-permute-start | bytes 2064392 | tf_op jit(solution)/shard_map/ppermute | solution.py:89
  42.9 24.3 %collective-permute-start.2 = (bf16[21,128,128]{2,1,0:T(8,128)(2,1)}, bf16[21,128,128]{2,1,0:T(8,128)(2,1)}, u32[]{:S(2)}, u32[]{:S(2)}) collective-permute-start(bf16[21,128,128]{2,1,0:T(8,128)(2,1)} %collective-permute-done.1.refs_7_.refs_12_), channel_id=1, source_target_pairs={{0,8},{8,0},{16,24},{24,16},{32,40},{40,32},{48,56},{56,48},{64,72... | collective-permute-start | bytes 2064392 | tf_op jit(solution)/shard_map/ppermute | solution.py:89
  47.7 19.6 %collective-permute-start.8 = (bf16[21,128,128]{2,1,0:T(8,128)(2,1)}, bf16[21,128,128]{2,1,0:T(8,128)(2,1)}, u32[]{:S(2)}, u32[]{:S(2)}) collective-permute-start(bf16[21,128,128]{2,1,0:T(8,128)(2,1)} %collective-permute-done.7.refs_13_.refs_18_), channel_id=1, source_target_pairs={{0,8},{8,0},{16,24},{24,16},{32,40},{40,32},{48,56},{56,48},{64,72... | collective-permute-start | bytes 2064392 | tf_op jit(solution)/shard_map/ppermute | solution.py:89
  48.6 26.6 %collective-permute-start.12 = (bf16[21,128,128]{2,1,0:T(8,128)(2,1)S(1)}, bf16[21,128,128]{2,1,0:T(8,128)(2,1)}, u32[]{:S(2)}, u32[]{:S(2)}) collective-permute-start(bf16[21,128,128]{2,1,0:T(8,128)(2,1)S(1)} %collective-permute-done.11.refs_9_.refs_17_.refs_22_), channel_id=1, source_target_pairs={{0,8},{8,0},{16,24},{24,16},{32,40},{40,32},{48,56},{56,48},{64,72... | collective-permute-start | bytes 2064392 | tf_op jit(solution)/shard_map/ppermute | solution.py:89
  49.9 25.3 %collective-permute-start.10 = (bf16[21,128,128]{2,1,0:T(8,128)(2,1)}, bf16[21,128,128]{2,1,0:T(8,128)(2,1)}, u32[]{:S(2)}, u32[]{:S(2)}) collective-permute-start(bf16[21,128,128]{2,1,0:T(8,128)(2,1)} %collective-permute-done.9.refs_7_.refs_15_.refs_20_), channel_id=1, source_target_pairs={{0,8},{8,0},{16,24},{24,16},{32,40},{40,32},{48,56},{56,48},{64,72... | collective-permute-start | bytes 2064392 | tf_op jit(solution)/shard_map/ppermute | solution.py:89
  55.9 19.3 %collective-permute-start.14 = (bf16[21,128,128]{2,1,0:T(8,128)(2,1)}, bf16[21,128,128]{2,1,0:T(8,128)(2,1)}, u32[]{:S(2)}, u32[]{:S(2)}) collective-permute-start(bf16[21,128,128]{2,1,0:T(8,128)(2,1)} %collective-permute-done.13.refs_11_.refs_19_.refs_24_), channel_id=1, source_target_pairs={{0,8},{8,0},{16,24},{24,16},{32,40},{40,32},{48,56},{56,48},{64,72... | collective-permute-start | bytes 2064392 | tf_op jit(solution)/shard_map/ppermute | solution.py:89
  86.7 8.5 %collective-permute-start.18 = (bf16[4,21,128,128]{3,2,1,0:T(8,128)(2,1)S(1)}, bf16[4,21,128,128]{3,2,1,0:T(8,128)(2,1)S(1)}, u32[]{:S(2)}, u32[]{:S(2)}) collective-permute-start(bf16[4,21,128,128]{3,2,1,0:T(8,128)(2,1)S(1)} %get-tuple-element.48), channel_id=1, source_target_pairs={{0,8},{8,0},{16,24},{24,16},{32,40},{40,32},{48,56},{56,48},{64,72... | collective-permute-start | bytes 8257544 | tf_op jit(solution)/shard_map/ppermute | solution.py:89
  95.1 52.6 %collective-permute-start.17 = (bf16[4,21,128,128]{3,2,1,0:T(8,128)(2,1)}, bf16[4,21,128,128]{3,2,1,0:T(8,128)(2,1)}, u32[]{:S(2)}, u32[]{:S(2)}) collective-permute-start(bf16[4,21,128,128]{3,2,1,0:T(8,128)(2,1)} %get-tuple-element.46), channel_id=1, source_target_pairs={{0,8},{8,0},{16,24},{24,16},{32,40},{40,32},{48,56},{56,48},{64,72... | collective-permute-start | bytes 8257544 | tf_op jit(solution)/shard_map/ppermute | solution.py:89
  96.8 51.4 %collective-permute-start.19 = (bf16[21,128,128]{2,1,0:T(8,128)(2,1)}, bf16[21,128,128]{2,1,0:T(8,128)(2,1)}, u32[]{:S(2)}, u32[]{:S(2)}) collective-permute-start(bf16[21,128,128]{2,1,0:T(8,128)(2,1)} %get-tuple-element.71), channel_id=1, source_target_pairs={{0,16},{8,24},{16,0},{24,8},{32,48},{40,56},{48,32},{56,40},{64,80... | collective-permute-start | bytes 2064392 | tf_op jit(solution)/shard_map/ppermute | solution.py:89
  101.6 60.3 %collective-permute-start.24 = (bf16[2,21,128,128]{3,2,1,0:T(8,128)(2,1)}, bf16[2,21,128,128]{3,2,1,0:T(8,128)(2,1)}, u32[]{:S(2)}, u32[]{:S(2)}) collective-permute-start(bf16[2,21,128,128]{3,2,1,0:T(8,128)(2,1)} %add_convert_fusion), channel_id=1, source_target_pairs={{0,96},{8,40},{16,112},{24,56},{32,0},{40,72},{48,16},{56,88},{64,... | collective-permute-start | bytes 4128776 | tf_op jit(solution)/shard_map/ppermute | solution.py:89
  114.8 13.2 %copy-start.25 = (bf16[14,192,128]{2,1,0:T(8,128)(2,1)S(1)}, bf16[14,192,128]{2,1,0:T(8,128)(2,1)}, u32[]{:S(2)}) copy-start(bf16[14,192,128]{2,1,0:T(8,128)(2,1)} %copy-done.24) | copy-start | bytes 2064388
  127.9 12.8 %collective-permute-start.31 = (f32[40,128]{1,0:T(8,128)S(1)}, f32[40,128]{1,0:T(8,128)S(1)}, u32[]{:S(2)}, u32[]{:S(2)}) collective-permute-start(f32[40,128]{1,0:T(8,128)S(1)} %get-tuple-element.63), channel_id=1, source_target_pairs={{0,8},{8,0},{16,24},{24,16},{32,40},{40,32},{48,56},{56,48},{64,72... | collective-permute-start | bytes 61448 | tf_op jit(solution)/shard_map/ppermute | solution.py:89
  139.2 11.0 %collective-permute-start.15 = (bf16[2,192,512]{2,1,0:T(8,128)(2,1)}, bf16[2,192,512]{2,1,0:T(8,128)(2,1)S(1)}, u32[]{:S(2)}, u32[]{:S(2)}) collective-permute-start(bf16[2,192,512]{2,1,0:T(8,128)(2,1)} %get-tuple-element.43), channel_id=1, source_target_pairs={{0,2},{1,3},{2,4},{3,5},{4,6},{5,7},{6,0},{7,1},{8,14},{9,15},{10,... | collective-permute-start | bytes 1179656 | tf_op jit(solution)/shard_map/ppermute | solution.py:93
  140.7 5.4 %collective-permute-start.32 = (f32[40,128]{1,0:T(8,128)S(1)}, f32[40,128]{1,0:T(8,128)S(1)}, u32[]{:S(2)}, u32[]{:S(2)}) collective-permute-start(f32[40,128]{1,0:T(8,128)S(1)} %add.260), channel_id=1, source_target_pairs={{0,16},{8,24},{16,0},{24,8},{32,48},{40,56},{48,32},{56,40},{64,80... | collective-permute-start | bytes 61448 | tf_op jit(solution)/shard_map/ppermute | solution.py:89
  146.1 34.2 %collective-permute-start.21 = (bf16[2,192,512]{2,1,0:T(8,128)(2,1)}, bf16[2,192,512]{2,1,0:T(8,128)(2,1)S(1)}, u32[]{:S(2)}, u32[]{:S(2)}) collective-permute-start(bf16[2,192,512]{2,1,0:T(8,128)(2,1)} %copy-done.39), channel_id=1, source_target_pairs={{0,6},{1,7},{2,0},{3,1},{4,2},{5,3},{6,4},{7,5},{8,10},{9,11},{10,... | collective-permute-start | bytes 1179656 | tf_op jit(solution)/shard_map/ppermute | solution.py:93
  147.8 11.3 %collective-permute-start.27 = (bf16[2,208,512]{2,1,0:T(8,128)(2,1)}, bf16[2,208,512]{2,1,0:T(8,128)(2,1)S(1)}, u32[]{:S(2)}, u32[]{:S(2)}) collective-permute-start(bf16[2,208,512]{2,1,0:T(8,128)(2,1)} %copy-done.38), channel_id=1, source_target_pairs={{0,2},{1,3},{2,4},{3,5},{4,6},{5,7},{6,0},{7,1},{8,14},{9,15},{10,... | collective-permute-start | bytes 1277960 | tf_op jit(solution)/shard_map/ppermute | solution.py:93
  148.2 12.4 %collective-permute-start.25 = (bf16[21,128,128]{2,1,0:T(8,128)(2,1)}, bf16[21,128,128]{2,1,0:T(8,128)(2,1)S(1)}, u32[]{:S(2)}, u32[]{:S(2)}) collective-permute-start(bf16[21,128,128]{2,1,0:T(8,128)(2,1)} %get-tuple-element.70), channel_id=1, source_target_pairs={{0,32},{8,104},{16,48},{24,120},{32,64},{40,8},{48,80},{56,24},{64... | collective-permute-start | bytes 2064392 | tf_op jit(solution)/shard_map/ppermute | solution.py:89
  148.2 10.9 %copy-start.37 = (bf16[2,208,512]{2,1,0:T(8,128)(2,1)S(1)}, bf16[2,208,512]{2,1,0:T(8,128)(2,1)}, u32[]{:S(2)}) copy-start(bf16[2,208,512]{2,1,0:T(8,128)(2,1)} %copy-done.36) | copy-start | bytes 1277956
  148.2 15.0 %copy-start.23 = (bf16[4,21,128,128]{3,2,1,0:T(8,128)(2,1)S(1)}, bf16[4,21,128,128]{3,2,1,0:T(8,128)(2,1)}, u32[]{:S(2)}) copy-start(bf16[4,21,128,128]{3,2,1,0:T(8,128)(2,1)} %copy-done.22) | copy-start | bytes 8257540
  150.2 17.7 %collective-permute-start.20 = (bf16[21,128,128]{2,1,0:T(8,128)(2,1)S(1)}, bf16[21,128,128]{2,1,0:T(8,128)(2,1)S(1)}, u32[]{:S(2)}, u32[]{:S(2)}) collective-permute-start(bf16[21,128,128]{2,1,0:T(8,128)(2,1)S(1)} %fusion.1), channel_id=1, source_target_pairs={{0,32},{8,104},{16,48},{24,120},{32,64},{40,8},{48,80},{56,24},{64... | collective-permute-start | bytes 2064392 | tf_op jit(solution)/shard_map/ppermute | solution.py:89
  159.1 20.1 %collective-permute-start.29 = (bf16[2,208,512]{2,1,0:T(8,128)(2,1)S(1)}, bf16[2,208,512]{2,1,0:T(8,128)(2,1)S(1)}, u32[]{:S(2)}, u32[]{:S(2)}) collective-permute-start(bf16[2,208,512]{2,1,0:T(8,128)(2,1)S(1)} %copy-done.37), channel_id=1, source_target_pairs={{0,6},{1,7},{2,0},{3,1},{4,2},{5,3},{6,4},{7,5},{8,10},{9,11},{10,... | collective-permute-start | bytes 1277960 | tf_op jit(solution)/shard_map/ppermute | solution.py:93
  160.5 18.6 %collective-permute-start.16 = (bf16[2,192,512]{2,1,0:T(8,128)(2,1)S(1)}, bf16[2,192,512]{2,1,0:T(8,128)(2,1)S(1)}, u32[]{:S(2)}, u32[]{:S(2)}) collective-permute-start(bf16[2,192,512]{2,1,0:T(8,128)(2,1)S(1)} %add_convert_fusion.4), channel_id=1, source_target_pairs={{0,2},{1,3},{2,4},{3,5},{4,6},{5,7},{6,0},{7,1},{8,14},{9,15},{10,... | collective-permute-start | bytes 1179656 | tf_op jit(solution)/shard_map/ppermute | solution.py:93
  162.0 13.9 %collective-permute-start.28 = (bf16[2,208,512]{2,1,0:T(8,128)(2,1)S(1)}, bf16[2,208,512]{2,1,0:T(8,128)(2,1)S(1)}, u32[]{:S(2)}, u32[]{:S(2)}) collective-permute-start(bf16[2,208,512]{2,1,0:T(8,128)(2,1)S(1)} %add_convert_fusion.3), channel_id=1, source_target_pairs={{0,2},{1,3},{2,4},{3,5},{4,6},{5,7},{6,0},{7,1},{8,14},{9,15},{10,... | collective-permute-start | bytes 1277960 | tf_op jit(solution)/shard_map/ppermute | solution.py:93
  164.9 15.2 %copy-start.27 = (bf16[2,208,512]{2,1,0:T(8,128)(2,1)S(1)}, bf16[2,208,512]{2,1,0:T(8,128)(2,1)}, u32[]{:S(2)}) copy-start(bf16[2,208,512]{2,1,0:T(8,128)(2,1)} %copy-done.26) | copy-start | bytes 1277956
  167.9 7.9 %collective-permute-start.33 = (f32[40,128]{1,0:T(8,128)S(1)}, f32[40,128]{1,0:T(8,128)S(1)}, u32[]{:S(2)}, u32[]{:S(2)}) collective-permute-start(f32[40,128]{1,0:T(8,128)S(1)} %add.261), channel_id=1, source_target_pairs={{0,1},{1,0},{2,3},{3,2},{4,5},{5,4},{6,7},{7,6},{8,9},{9,8},{10,11... | collective-permute-start | bytes 61448 | tf_op jit(solution)/shard_map/ppermute | solution.py:93
  169.3 11.4 %copy-start.31 = (bf16[2,192,512]{2,1,0:T(8,128)(2,1)S(1)}, bf16[2,192,512]{2,1,0:T(8,128)(2,1)}, u32[]{:S(2)}) copy-start(bf16[2,192,512]{2,1,0:T(8,128)(2,1)} %copy-done.30) | copy-start | bytes 1179652
  175.9 21.1 %collective-permute-start.23 = (bf16[21,128,128]{2,1,0:T(8,128)(2,1)S(1)}, bf16[21,128,128]{2,1,0:T(8,128)(2,1)S(1)}, u32[]{:S(2)}, u32[]{:S(2)}) collective-permute-start(bf16[21,128,128]{2,1,0:T(8,128)(2,1)S(1)} %fusion.2), channel_id=1, source_target_pairs={{0,32},{8,104},{16,48},{24,120},{32,64},{40,8},{48,80},{56,24},{64... | collective-permute-start | bytes 2064392 | tf_op jit(solution)/shard_map/ppermute | solution.py:89
  175.9 12.8 %collective-permute-start.36 = (f32[40,128]{1,0:T(8,128)S(1)}, f32[40,128]{1,0:T(8,128)S(1)}, u32[]{:S(2)}, u32[]{:S(2)}) collective-permute-start(f32[40,128]{1,0:T(8,128)S(1)} %add.262), channel_id=1, source_target_pairs={{0,96},{8,104},{16,112},{24,120},{32,64},{40,72},{48,80},{56,88},{... | collective-permute-start | bytes 61448 | tf_op jit(solution)/shard_map/ppermute | solution.py:89
  179.2 9.5 %collective-permute-start.35 = (f32[40,128]{1,0:T(8,128)S(1)}, f32[40,128]{1,0:T(8,128)S(1)}, u32[]{:S(2)}, u32[]{:S(2)}) collective-permute-start(f32[40,128]{1,0:T(8,128)S(1)} %add.262), channel_id=1, source_target_pairs={{0,64},{8,72},{16,80},{24,88},{32,96},{40,104},{48,112},{56,120},{... | collective-permute-start | bytes 61448 | tf_op jit(solution)/shard_map/ppermute | solution.py:89
  179.2 9.5 %collective-permute-start.34 = (f32[40,128]{1,0:T(8,128)S(1)}, f32[40,128]{1,0:T(8,128)S(1)}, u32[]{:S(2)}, u32[]{:S(2)}) collective-permute-start(f32[40,128]{1,0:T(8,128)S(1)} %add.262), channel_id=1, source_target_pairs={{0,32},{8,40},{16,48},{24,56},{32,0},{40,8},{48,16},{56,24},{64,96... | collective-permute-start | bytes 61448 | tf_op jit(solution)/shard_map/ppermute | solution.py:89
  180.3 19.9 %collective-permute-start.26 = (bf16[21,128,128]{2,1,0:T(8,128)(2,1)S(1)}, bf16[21,128,128]{2,1,0:T(8,128)(2,1)S(1)}, u32[]{:S(2)}, u32[]{:S(2)}) collective-permute-start(bf16[21,128,128]{2,1,0:T(8,128)(2,1)S(1)} %fusion), channel_id=1, source_target_pairs={{0,16},{8,24},{16,0},{24,8},{32,48},{40,56},{48,32},{56,40},{64,80... | collective-permute-start | bytes 2064392 | tf_op jit(solution)/shard_map/ppermute | solution.py:89
  188.7 5.1 %collective-permute-start.39 = (f32[40,128]{1,0:T(8,128)S(1)}, f32[40,128]{1,0:T(8,128)S(1)}, u32[]{:S(2)}, u32[]{:S(2)}) collective-permute-start(f32[40,128]{1,0:T(8,128)S(1)} %add_add_fusion.1), channel_id=1, source_target_pairs={{0,6},{1,7},{2,4},{3,5},{4,2},{5,3},{6,0},{7,1},{8,14},{9,15},{10,... | collective-permute-start | bytes 61448 | tf_op jit(solution)/shard_map/ppermute | solution.py:93
  190.5 5.3 %collective-permute-start.38 = (f32[40,128]{1,0:T(8,128)S(1)}, f32[40,128]{1,0:T(8,128)S(1)}, u32[]{:S(2)}, u32[]{:S(2)}) collective-permute-start(f32[40,128]{1,0:T(8,128)S(1)} %add_add_fusion.1), channel_id=1, source_target_pairs={{0,4},{1,5},{2,6},{3,7},{4,0},{5,1},{6,2},{7,3},{8,12},{9,13},{10,... | collective-permute-start | bytes 61448 | tf_op jit(solution)/shard_map/ppermute | solution.py:93
  190.5 5.3 %collective-permute-start.37 = (f32[40,128]{1,0:T(8,128)S(1)}, f32[40,128]{1,0:T(8,128)S(1)}, u32[]{:S(2)}, u32[]{:S(2)}) collective-permute-start(f32[40,128]{1,0:T(8,128)S(1)} %add_add_fusion.1), channel_id=1, source_target_pairs={{0,2},{1,3},{2,0},{3,1},{4,6},{5,7},{6,4},{7,5},{8,10},{9,11},{10,... | collective-permute-start | bytes 61448 | tf_op jit(solution)/shard_map/ppermute | solution.py:93
  193.8 9.7 %collective-permute-start.22 = (bf16[192,512]{1,0:T(8,128)(2,1)S(1)}, bf16[192,512]{1,0:T(8,128)(2,1)S(1)}, u32[]{:S(2)}, u32[]{:S(2)}) collective-permute-start(bf16[192,512]{1,0:T(8,128)(2,1)S(1)} %fusion.15), channel_id=1, source_target_pairs={{0,1},{1,0},{2,3},{3,2},{4,5},{5,4},{6,7},{7,6},{8,9},{9,8},{10,11... | collective-permute-start | bytes 589832 | tf_op jit(solution)/shard_map/ppermute | solution.py:93
  195.8 7.6 %collective-permute-start.30 = (bf16[208,512]{1,0:T(8,128)(2,1)S(1)}, bf16[208,512]{1,0:T(8,128)(2,1)S(1)}, u32[]{:S(2)}, u32[]{:S(2)}) collective-permute-start(bf16[208,512]{1,0:T(8,128)(2,1)S(1)} %fusion.14), channel_id=1, source_target_pairs={{0,1},{1,0},{2,3},{3,2},{4,5},{5,4},{6,7},{7,6},{8,9},{9,8},{10,11... | collective-permute-start | bytes 638984 | tf_op jit(solution)/shard_map/ppermute | solution.py:93
  (36 other events, 146.7 us)

commit v2 on v1

--- a/solution.py
+++ b/solution.py
@@ -560,9 +560,12 @@
     return sum(v.astype(F32) for v in values)
 
 
-def reduce_tensor(pieces, after, last):
+def reduce_tensor(pieces, after, last, first=None):
     own, to_a, to_b, far = pieces
-    near = add(to_a, over_tensor(far, "a")).astype(BF)
+    from_far = over_tensor(far, "a")
+    if first is not None:
+        from_far, _ = barrier(from_far, first)
+    near = add(to_a, from_far).astype(BF)
     from_a, _ = barrier(over_tensor(near, "a"), after)
     total = add(own, from_a, over_tensor(to_b, "b"))
     moved, _ = barrier(over_tensor(total[1].astype(BF), "y"), last)
@@ -664,7 +667,7 @@
         add(*[v[k * share : (k + 1) * share] for v in (own1, own2, near_a, near_b, across)]) for k in range(3)
     ]
 
-    back = reduce_tensor(back_pieces, near, block_grads[0])
+    back = reduce_tensor(back_pieces, near, block_grads[0], across_low)
     ffn = reduce_tensor(out_pieces, near, block_grads[0])
     small = reduce_small(small, across_low)
 

time: 207 us -> 213 us (1.029)
  starting transfers between devices: 44.2 us -> 47.9 us
  other arithmetic: 13.9 us -> 16.7 us
  waiting for transfers between devices: 66.3 us -> 68.9 us
  local copies, waits for them, and re-layouts: 24.9 us -> 22.6 us
    ppermute x12, starting transfers between devices: 10.4 us -> 14 us  [over_tensor(): return lax.ppermute(value, ('dp', 'tensor'), tensor_perm(kind))]
    ppermute x12, waiting for transfers between devices: 17 us -> 19.7 us  [over_tensor(): return lax.ppermute(value, ('dp', 'tensor'), tensor_perm(kind))]
    unnamed x88, local copies, waits for them, and re-layouts: 23.7 us -> 21.4 us
  transfers between devices with their start and end apart: 40 -> 40, of which waited for: 15 -> 12; matrix products, arithmetic and copies ran while one was open for 6% -> 8% of each run, Pallas kernels for 20% -> 19%
where the time goes in v2:
time: 213 us; the launch traced here: 212 us
  waiting for transfers between devices  68.9 us (32%)
  Pallas kernels  54.8 us (26%)
  starting transfers between devices  47.9 us (22%)
  local copies, waits for them, and re-layouts  22.6 us (11%)
  other arithmetic  16.7 us (8%)
    ppermute x28, waiting for transfers between devices, over_dp(): return lax.ppermute(value, 'dp', dp_perm(kind))  49.2 us
    ppermute x28, starting transfers between devices, over_dp(): return lax.ppermute(value, 'dp', dp_perm(kind))  33.9 us
    unnamed x88, local copies, waits for them, and re-layouts  21.4 us
    ppermute x12, waiting for transfers between devices, over_tensor(): return lax.ppermute(value, ('dp', 'tensor'), tensor_perm(kind))  19.7 us
    ppermute x12, starting transfers between devices, over_tensor(): return lax.ppermute(value, ('dp', 'tensor'), tensor_perm(kind))  14 us
    pallas_call x1, Pallas kernels, input_call(): pl.pallas_call(functools.partial(input_kernel, share), out_shape=(piece,)...  13 us
    pallas_call x1, Pallas kernels, late_call(): pl.pallas_call(functools.partial(late_kernel, share, count), out_shape=(j...  11.4 us
    pallas_call x1, Pallas kernels, output_call(): pl.pallas_call(functools.partial(output_kernel, share), out_shape=(piece,...  8.85 us
  transfers between devices with their start and end apart: 40, of which 12 were waited for; matrix products, arithmetic and copies ran while one was open for 8% of the time, Pallas kernels for 19%

profile of v2, /device:TPU:0, one launch (start us, length us, event | category | flops | bytes accessed | tf_op | source)
XLA Modules:
  0.0 212.2 jit_solution(15765980264072079989)
XLA Ops:
  0.7 2.0 join.1.refs_5_.refs_10_
  2.7 2.1 collective-permute-start.1
  4.8 3.2 %collective-permute-start.5 = (bf16[21,128,128]{2,1,0:T(8,128)(2,1)}, bf16[21,128,128]{2,1,0:T(8,128)(2,1)S(1)}, u32[]{:S(2)}, u32[]{:S(2)}) collective-permute-start(bf16[21,128,128]{2,1,0:T(8,128)(2,1)} %join.1.refs_5_.refs_10_), channel_id=1, source_target_pairs={{0,16},{8,24},{16,0},{24,8},{32,48},{40,56},{48,32},{56,40},{64,80... | collective-permute-start | bytes 2064392 | tf_op jit(solution)/shard_map/ppermute | solution.py:89
  8.0 2.2 %collective-permute-start.3 = (bf16[21,128,128]{2,1,0:T(8,128)(2,1)}, bf16[21,128,128]{2,1,0:T(8,128)(2,1)S(1)}, u32[]{:S(2)}, u32[]{:S(2)}) collective-permute-start(bf16[21,128,128]{2,1,0:T(8,128)(2,1)} %join.1.refs_5_.refs_10_), channel_id=1, source_target_pairs={{0,96},{8,40},{16,112},{24,56},{32,0},{40,72},{48,16},{56,88},{64,... | collective-permute-start | bytes 2064392 | tf_op jit(solution)/shard_map/ppermute | solution.py:89
  10.2 8.6 %collective-permute-done.1.refs_7_.refs_12_ = bf16[21,128,128]{2,1,0:T(8,128)(2,1)} collective-permute-done((bf16[21,128,128]{2,1,0:T(8,128)(2,1)}, bf16[21,128,128]{2,1,0:T(8,128)(2,1)}, u32[]{:S(2)}, u32[]{:S(2)}) %collective-permute-start.1) | collective-permute-done | bytes 688160 | tf_op jit(solution)/shard_map/ppermute | solution.py:89
  18.8 2.2 %collective-permute-start.7 = (bf16[21,128,128]{2,1,0:T(8,128)(2,1)}, bf16[21,128,128]{2,1,0:T(8,128)(2,1)}, u32[]{:S(2)}, u32[]{:S(2)}) collective-permute-start(bf16[21,128,128]{2,1,0:T(8,128)(2,1)} %collective-permute-done.1.refs_7_.refs_12_), channel_id=1, source_target_pairs={{0,32},{8,104},{16,48},{24,120},{32,64},{40,8},{48,80},{56,24},{64... | collective-permute-start | bytes 2064392 | tf_op jit(solution)/shard_map/ppermute | solution.py:89
  21.0 3.1 %collective-permute-done.5.refs_11_.refs_16_ = bf16[21,128,128]{2,1,0:T(8,128)(2,1)S(1)} collective-permute-done((bf16[21,128,128]{2,1,0:T(8,128)(2,1)}, bf16[21,128,128]{2,1,0:T(8,128)(2,1)S(1)}, u32[]{:S(2)}, u32[]{:S(2)}) %collective-permute-start.5) | collective-permute-done | bytes 688160 | tf_op jit(solution)/shard_map/ppermute | solution.py:89
  24.1 1.8 collective-permute-start.11
  26.2 1.2 collective-permute-start.6
  29.9 7.3 %collective-permute-done.7.refs_13_.refs_18_ = bf16[21,128,128]{2,1,0:T(8,128)(2,1)} collective-permute-done((bf16[21,128,128]{2,1,0:T(8,128)(2,1)}, bf16[21,128,128]{2,1,0:T(8,128)(2,1)}, u32[]{:S(2)}, u32[]{:S(2)}) %collective-permute-start.7) | collective-permute-done | bytes 688160 | tf_op jit(solution)/shard_map/ppermute | solution.py:89
  37.2 5.7 %collective-permute-start.13 = (bf16[21,128,128]{2,1,0:T(8,128)(2,1)}, bf16[21,128,128]{2,1,0:T(8,128)(2,1)}, u32[]{:S(2)}, u32[]{:S(2)}) collective-permute-start(bf16[21,128,128]{2,1,0:T(8,128)(2,1)} %collective-permute-done.7.refs_13_.refs_18_), channel_id=1, source_target_pairs={{0,16},{8,24},{16,0},{24,8},{32,48},{40,56},{48,32},{56,40},{64,80... | collective-permute-start | bytes 2064392 | tf_op jit(solution)/shard_map/ppermute | solution.py:89
  43.4 4.2 %collective-permute-done.9.refs_7_.refs_15_.refs_20_ = bf16[21,128,128]{2,1,0:T(8,128)(2,1)} collective-permute-done((bf16[21,128,128]{2,1,0:T(8,128)(2,1)S(1)}, bf16[21,128,128]{2,1,0:T(8,128)(2,1)}, u32[]{:S(2)}, u32[]{:S(2)}) %collective-permute-start.9) | collective-permute-done | bytes 688160 | tf_op jit(solution)/shard_map/ppermute | solution.py:89
  49.9 6.0 %collective-permute-done.13.refs_11_.refs_19_.refs_24_ = bf16[21,128,128]{2,1,0:T(8,128)(2,1)} collective-permute-done((bf16[21,128,128]{2,1,0:T(8,128)(2,1)}, bf16[21,128,128]{2,1,0:T(8,128)(2,1)}, u32[]{:S(2)}, u32[]{:S(2)}) %collective-permute-start.13) | collective-permute-done | bytes 688160 | tf_op jit(solution)/shard_map/ppermute | solution.py:89
  55.9 2.8 %copy-done = bf16[4,192,4096]{2,1,0:T(8,128)(2,1)S(1)} copy-done((bf16[4,192,4096]{2,1,0:T(8,128)(2,1)S(1)}, bf16[4,192,4096]{2,1,0:T(8,128)(2,1)}, u32[]{:S(2)}) %copy-start) | copy-done | bytes 6291480
  58.7 1.4 copy-done.2
  60.1 5.3 %norm.1 = (bf16[192,4096]{1,0:T(8,128)(2,1)S(1)}, f32[192,128]{1,0:T(8,128)S(1)}, f32[192,4096]{1,0:T(8,128)S(1)}) custom-call(s32[4]{0:T(128)S(1)} %copy-done.33, f32[4]{0:T(128)S(1)} %copy-done.34, bf16[4,192,4096]{2,1,0:T(8,128)(2,1)S(1)} %copy-done, bf16[4,192,4096]{2,1,0:T(8,128)(2,1)S(1)} %copy-done, bf16[4,192,4096]{2,1,0:T(8,128)(2,1)S(1)} %copy-done, ...), custom_call_target="tpu_custom_call" | custom-call | flops 23592960 | bytes 9437184 | tf_op jit(solution)/shard_map/norm/pallas_call | solution.py:161
  65.5 1.6 copy-done.32
  67.3 7.8 %early.1 = (f32[14,192,256]{2,1,0:T(8,128)S(1)}, f32[14,192,128]{2,1,0:T(8,128)S(1)}) custom-call(s32[32]{0:T(128)S(1)} %fusion.21.refs_0_.table, s32[112]{0:T(128)S(1)} %get-tuple-element.77.refs_1_.rows, s32[112]{0:T(128)S(1)} %get-tuple-element.76.refs_2_.cols, bf16[192,4096]{1,0:T(8,128)(2,1)S(1)} %get-tuple-element.38.refs_3_.normed, ...), custom_call_target="tpu_custom_call" | custom-call | flops 1056964608 | bytes 12000000 | tf_op jit(solution)/shard_map/early/pallas_call | solution.py:303
  75.2 11.4 %late.1 = (bf16[14,192,128]{2,1,0:T(8,128)(2,1)S(1)}, bf16[14,192,256]{2,1,0:T(8,128)(2,1)S(1)}, bf16[4,21,128,128]{3,2,1,0:T(8,128)(2,1)S(1)}, bf16[4,21,128,128]{3,2,1,0:T(8,128)(2,1)S(1)}) custom-call(s32[32]{0:T(128)S(1)} %fusion.21.refs_0_.table, s32[112]{0:T(128)S(1)} %get-tuple-element.77.refs_1_.rows, s32[112]{0:T(128)S(1)} %get-tuple-element.76.refs_2_.cols, ...), custom_call_target="tpu_custom_call" | custom-call | flops 2113929216 | bytes 20000000 | tf_op jit(solution)/shard_map/late/pallas_call | solution.py:356
  87.2 6.3 %rest.1 = (bf16[4,21,128,128]{3,2,1,0:T(8,128)(2,1)S(1)}, bf16[4,21,128,128]{3,2,1,0:T(8,128)(2,1)}) custom-call(s32[32]{0:T(128)S(1)} %fusion.21.refs_0_.table, s32[112]{0:T(128)S(1)} %get-tuple-element.77.refs_1_.rows, s32[112]{0:T(128)S(1)} %get-tuple-element.76.refs_2_.cols, bf16[192,4096]{1,0:T(8,128)(2,1)S(1)} %get-tuple-element.38.refs_3_.normed, ...), custom_call_target="tpu_custom_call" | custom-call | flops 1056964608 | bytes 10000000 | tf_op jit(solution)/shard_map/rest/pallas_call | solution.py:390
  93.5 1.6 copy-done.22
  95.1 1.8 add_convert_fusion
  96.9 3.6 %collective-permute-start.24 = (bf16[2,21,128,128]{3,2,1,0:T(8,128)(2,1)}, bf16[2,21,128,128]{3,2,1,0:T(8,128)(2,1)}, u32[]{:S(2)}, u32[]{:S(2)}) collective-permute-start(bf16[2,21,128,128]{3,2,1,0:T(8,128)(2,1)} %add_convert_fusion), channel_id=1, source_target_pairs={{0,96},{8,40},{16,112},{24,56},{32,0},{40,72},{48,16},{56,88},{64,... | collective-permute-start | bytes 4128776 | tf_op jit(solution)/shard_map/ppermute | solution.py:89
  100.5 1.8 fusion.4
  102.2 3.2 %collective-permute-start.19 = (bf16[21,128,128]{2,1,0:T(8,128)(2,1)}, bf16[21,128,128]{2,1,0:T(8,128)(2,1)}, u32[]{:S(2)}, u32[]{:S(2)}) collective-permute-start(bf16[21,128,128]{2,1,0:T(8,128)(2,1)} %get-tuple-element.73), channel_id=1, source_target_pairs={{0,16},{8,24},{16,0},{24,8},{32,48},{40,56},{48,32},{56,40},{64,80... | collective-permute-start | bytes 2064392 | tf_op jit(solution)/shard_map/ppermute | solution.py:89
  105.5 2.8 %copy-done.1 = bf16[4,192,4096]{2,1,0:T(8,128)(2,1)S(1)} copy-done((bf16[4,192,4096]{2,1,0:T(8,128)(2,1)S(1)}, bf16[4,192,4096]{2,1,0:T(8,128)(2,1)}, u32[]{:S(2)}) %copy-start.1) | copy-done | bytes 6291480
  108.3 1.1 copy-done.7
  113.8 1.3 copy-done.21
  115.1 13.0 %input_grad.1 = (bf16[2,208,512]{2,1,0:T(8,128)(2,1)S(1)}, bf16[2,208,512]{2,1,0:T(8,128)(2,1)S(1)}, bf16[2,208,512]{2,1,0:T(8,128)(2,1)S(1)}, bf16[2,208,512]{2,1,0:T(8,128)(2,1)S(1)}, f32[40,128]{1,0:T(8,128)S(1)}) custom-call(s32[32]{0:T(128)S(1)} %fusion.21.refs_0_.table, s32[112]{0:T(128)S(1)} %get-tuple-element.77.refs_1_.rows, ...), custom_call_target="tpu_custom_call" | custom-call | flops 1409286144 | bytes 20000000 | tf_op jit(solution)/shard_map/input_grad/pallas_call | solution.py:490
  128.3 8.8 %output.1 = (bf16[2,192,512]{2,1,0:T(8,128)(2,1)S(1)}, bf16[2,192,512]{2,1,0:T(8,128)(2,1)S(1)}, bf16[2,192,512]{2,1,0:T(8,128)(2,1)S(1)}, bf16[2,192,512]{2,1,0:T(8,128)(2,1)}) custom-call(s32[32]{0:T(128)S(1)} %fusion.21.refs_0_.table, s32[112]{0:T(128)S(1)} %get-tuple-element.77.refs_1_.rows, s32[112]{0:T(128)S(1)} %get-tuple-element.76.refs_2_.cols, ...), custom_call_target="tpu_custom_call" | custom-call | flops 704643072 | bytes 10000000 | tf_op jit(solution)/shard_map/output/pallas_call | solution.py:539
  137.2 1.6 collective-permute-start.15
  138.8 2.8 %fusion.1 = bf16[21,128,128]{2,1,0:T(8,128)(2,1)} fusion(bf16[21,128,128]{2,1,0:T(8,128)(2,1)} %collective-permute-done.19, bf16[4,21,128,128]{3,2,1,0:T(8,128)(2,1)} %collective-permute-done.17, bf16[4,21,128,128]{3,2,1,0:T(8,128)(2,1)} %copy-done.22), kind=kLoop, calls=%fused_computation.5 | loop fusion | flops 2064384 | bytes 2752512 | tf_op jit(solution)/shard_map/convert_element_type | solution.py:660
  141.7 1.3 collective-permute-start.20
  143.6 4.9 %collective-permute-done.32 = f32[40,128]{1,0:T(8,128)S(1)} collective-permute-done((f32[40,128]{1,0:T(8,128)S(1)}, f32[40,128]{1,0:T(8,128)S(1)}, u32[]{:S(2)}, u32[]{:S(2)}) %collective-permute-start.32) | collective-permute-done | bytes 20512 | tf_op jit(solution)/shard_map/ppermute | solution.py:89
  148.5 1.5 collective-permute-start.21
  151.8 2.8 %collective-permute-start.29 = (bf16[2,208,512]{2,1,0:T(8,128)(2,1)S(1)}, bf16[2,208,512]{2,1,0:T(8,128)(2,1)S(1)}, u32[]{:S(2)}, u32[]{:S(2)}) collective-permute-start(bf16[2,208,512]{2,1,0:T(8,128)(2,1)S(1)} %copy-done.36), channel_id=1, source_target_pairs={{0,6},{1,7},{2,0},{3,1},{4,2},{5,3},{6,4},{7,5},{8,10},{9,11},{10,... | collective-permute-start | bytes 1277960 | tf_op jit(solution)/shard_map/ppermute | solution.py:93
  154.6 2.2 %fusion = bf16[21,128,128]{2,1,0:T(8,128)(2,1)S(1)} fusion(bf16[21,128,128]{2,1,0:T(8,128)(2,1)} %collective-permute-done.25, bf16[2,21,128,128]{3,2,1,0:T(8,128)(2,1)} %collective-permute-done.24, bf16[4,21,128,128]{3,2,1,0:T(8,128)(2,1)} %collective-permute-done.17, bf16[4,21,128,128]{3,2,1,0:T(8,128)(2,1)} %copy-done.22), kind=kLoop, calls=%fused_computation.2 | loop fusion | flops 2752512 | bytes 3440640 | tf_op jit(solution)/shard_map/convert_element_type | solution.py:662
  156.9 1.6 fusion.2
  158.5 11.7 %collective-permute-done.16 = bf16[2,192,512]{2,1,0:T(8,128)(2,1)S(1)} collective-permute-done((bf16[2,192,512]{2,1,0:T(8,128)(2,1)S(1)}, bf16[2,192,512]{2,1,0:T(8,128)(2,1)S(1)}, u32[]{:S(2)}, u32[]{:S(2)}) %collective-permute-start.16) | collective-permute-done | bytes 393248 | tf_op jit(solution)/shard_map/ppermute | solution.py:93
  170.7 2.9 %collective-permute-start.36 = (f32[40,128]{1,0:T(8,128)S(1)}, f32[40,128]{1,0:T(8,128)S(1)}, u32[]{:S(2)}, u32[]{:S(2)}) collective-permute-start(f32[40,128]{1,0:T(8,128)S(1)} %add.262), channel_id=1, source_target_pairs={{0,96},{8,104},{16,112},{24,120},{32,64},{40,72},{48,80},{56,88},{... | collective-permute-start | bytes 61448 | tf_op jit(solution)/shard_map/ppermute | solution.py:89
  175.1 7.9 %collective-permute-done.36 = f32[40,128]{1,0:T(8,128)S(1)} collective-permute-done((f32[40,128]{1,0:T(8,128)S(1)}, f32[40,128]{1,0:T(8,128)S(1)}, u32[]{:S(2)}, u32[]{:S(2)}) %collective-permute-start.36) | collective-permute-done | bytes 20512 | tf_op jit(solution)/shard_map/ppermute | solution.py:89
  184.0 3.2 %collective-permute-start.37 = (f32[40,128]{1,0:T(8,128)S(1)}, f32[40,128]{1,0:T(8,128)S(1)}, u32[]{:S(2)}, u32[]{:S(2)}) collective-permute-start(f32[40,128]{1,0:T(8,128)S(1)} %add_add_fusion.1), channel_id=1, source_target_pairs={{0,2},{1,3},{2,0},{3,1},{4,6},{5,7},{6,4},{7,5},{8,10},{9,11},{10,... | collective-permute-start | bytes 61448 | tf_op jit(solution)/shard_map/ppermute | solution.py:93
  189.2 1.8 collective-permute-start.28
  192.1 6.4 %collective-permute-done.28 = bf16[2,208,512]{2,1,0:T(8,128)(2,1)S(1)} collective-permute-done((bf16[2,208,512]{2,1,0:T(8,128)(2,1)S(1)}, bf16[2,208,512]{2,1,0:T(8,128)(2,1)S(1)}, u32[]{:S(2)}, u32[]{:S(2)}) %collective-permute-start.28) | collective-permute-done | bytes 426016 | tf_op jit(solution)/shard_map/ppermute | solution.py:93
  198.7 1.4 collective-permute-start.30
  200.2 7.1 %collective-permute-done.26 = bf16[21,128,128]{2,1,0:T(8,128)(2,1)S(1)} collective-permute-done((bf16[21,128,128]{2,1,0:T(8,128)(2,1)S(1)}, bf16[21,128,128]{2,1,0:T(8,128)(2,1)S(1)}, u32[]{:S(2)}, u32[]{:S(2)}) %collective-permute-start.26) | collective-permute-done | bytes 688160 | tf_op jit(solution)/shard_map/ppermute | solution.py:89
  207.3 2.8 %fusion.5 = (f32[7,128,128]{2,1,0:T(8,128)}, f32[7,128,128]{2,1,0:T(8,128)}, f32[7,128,128]{2,1,0:T(8,128)}) fusion(bf16[21,128,128]{2,1,0:T(8,128)(2,1)S(1)} %collective-permute-done.26, bf16[2,21,128,128]{3,2,1,0:T(8,128)(2,1)} %collective-permute-done.24, bf16[21,128,128]{2,1,0:T(8,128)(2,1)S(1)} %collective-permute-done.23, ...), kind=kLoop, calls=%fused_computation.17 | loop fusion | flops 3096576 | bytes 4816896 | tf_op jit(solution)/shard_map/add | solution.py:560
  210.2 2.0 fusion.10
  (154 shorter events, 19.5 us)
Async XLA Ops:
  0.6 55.2 %copy-start.31 = (f32[4096]{0:T(1024)S(1)}, f32[4096]{0:T(1024)}, u32[]{:S(2)}) copy-start(f32[4096]{0:T(1024)} %param.15) | copy-start | bytes 49156
  0.6 55.2 %copy-start.33 = (s32[4]{0:T(128)S(1)}, s32[4]{0:T(128)}, u32[]{:S(2)}) copy-start(s32[4]{0:T(128)} %refs_4_.5) | copy-start | bytes 52
  0.7 55.2 %copy-start.34 = (f32[4]{0:T(128)S(1)}, f32[4]{0:T(128)}, u32[]{:S(2)}) copy-start(f32[4]{0:T(128)} %refs_5_.1) | copy-start | bytes 52
  2.7 16.1 %collective-permute-start.1 = (bf16[21,128,128]{2,1,0:T(8,128)(2,1)}, bf16[21,128,128]{2,1,0:T(8,128)(2,1)}, u32[]{:S(2)}, u32[]{:S(2)}) collective-permute-start(bf16[21,128,128]{2,1,0:T(8,128)(2,1)} %join.1.refs_5_.refs_10_), channel_id=1, source_target_pairs={{0,32},{8,104},{16,48},{24,120},{32,64},{40,8},{48,80},{56,24},{64... | collective-permute-start | bytes 2064392 | tf_op jit(solution)/shard_map/ppermute | solution.py:89
  4.8 19.3 %collective-permute-start.5 = (bf16[21,128,128]{2,1,0:T(8,128)(2,1)}, bf16[21,128,128]{2,1,0:T(8,128)(2,1)S(1)}, u32[]{:S(2)}, u32[]{:S(2)}) collective-permute-start(bf16[21,128,128]{2,1,0:T(8,128)(2,1)} %join.1.refs_5_.refs_10_), channel_id=1, source_target_pairs={{0,16},{8,24},{16,0},{24,8},{32,48},{40,56},{48,32},{56,40},{64,80... | collective-permute-start | bytes 2064392 | tf_op jit(solution)/shard_map/ppermute | solution.py:89
  8.0 18.1 %collective-permute-start.3 = (bf16[21,128,128]{2,1,0:T(8,128)(2,1)}, bf16[21,128,128]{2,1,0:T(8,128)(2,1)S(1)}, u32[]{:S(2)}, u32[]{:S(2)}) collective-permute-start(bf16[21,128,128]{2,1,0:T(8,128)(2,1)} %join.1.refs_5_.refs_10_), channel_id=1, source_target_pairs={{0,96},{8,40},{16,112},{24,56},{32,0},{40,72},{48,16},{56,88},{64,... | collective-permute-start | bytes 2064392 | tf_op jit(solution)/shard_map/ppermute | solution.py:89
  10.2 18.0 %collective-permute-start = (bf16[21,128,128]{2,1,0:T(8,128)(2,1)}, bf16[21,128,128]{2,1,0:T(8,128)(2,1)S(1)}, u32[]{:S(2)}, u32[]{:S(2)}) collective-permute-start(bf16[21,128,128]{2,1,0:T(8,128)(2,1)} %join.1.refs_5_.refs_10_), channel_id=1, source_target_pairs={{0,8},{8,0},{16,24},{24,16},{32,40},{40,32},{48,56},{56,48},{64,72... | collective-permute-start | bytes 2064392 | tf_op jit(solution)/shard_map/ppermute | solution.py:89
  18.8 18.4 %collective-permute-start.7 = (bf16[21,128,128]{2,1,0:T(8,128)(2,1)}, bf16[21,128,128]{2,1,0:T(8,128)(2,1)}, u32[]{:S(2)}, u32[]{:S(2)}) collective-permute-start(bf16[21,128,128]{2,1,0:T(8,128)(2,1)} %collective-permute-done.1.refs_7_.refs_12_), channel_id=1, source_target_pairs={{0,32},{8,104},{16,48},{24,120},{32,64},{40,8},{48,80},{56,24},{64... | collective-permute-start | bytes 2064392 | tf_op jit(solution)/shard_map/ppermute | solution.py:89
  24.1 18.8 %collective-permute-start.11 = (bf16[21,128,128]{2,1,0:T(8,128)(2,1)S(1)}, bf16[21,128,128]{2,1,0:T(8,128)(2,1)S(1)}, u32[]{:S(2)}, u32[]{:S(2)}) collective-permute-start(bf16[21,128,128]{2,1,0:T(8,128)(2,1)S(1)} %collective-permute-done.5.refs_11_.refs_16_), channel_id=1, source_target_pairs={{0,96},{8,40},{16,112},{24,56},{32,0},{40,72},{48,16},{56,88},{64,... | collective-permute-start | bytes 2064392 | tf_op jit(solution)/shard_map/ppermute | solution.py:89
  26.0 21.7 %collective-permute-start.9 = (bf16[21,128,128]{2,1,0:T(8,128)(2,1)S(1)}, bf16[21,128,128]{2,1,0:T(8,128)(2,1)}, u32[]{:S(2)}, u32[]{:S(2)}) collective-permute-start(bf16[21,128,128]{2,1,0:T(8,128)(2,1)S(1)} %collective-permute-done.5.refs_11_.refs_16_), channel_id=1, source_target_pairs={{0,32},{8,104},{16,48},{24,120},{32,64},{40,8},{48,80},{56,24},{64... | collective-permute-start | bytes 2064392 | tf_op jit(solution)/shard_map/ppermute | solution.py:89
  26.2 21.5 %collective-permute-start.6 = (bf16[21,128,128]{2,1,0:T(8,128)(2,1)S(1)}, bf16[21,128,128]{2,1,0:T(8,128)(2,1)S(1)}, u32[]{:S(2)}, u32[]{:S(2)}) collective-permute-start(bf16[21,128,128]{2,1,0:T(8,128)(2,1)S(1)} %collective-permute-done.5.refs_11_.refs_16_), channel_id=1, source_target_pairs={{0,8},{8,0},{16,24},{24,16},{32,40},{40,32},{48,56},{56,48},{64,72... | collective-permute-start | bytes 2064392 | tf_op jit(solution)/shard_map/ppermute | solution.py:89
  29.1 19.9 %collective-permute-start.4 = (bf16[21,128,128]{2,1,0:T(8,128)(2,1)S(1)}, bf16[21,128,128]{2,1,0:T(8,128)(2,1)S(1)}, u32[]{:S(2)}, u32[]{:S(2)}) collective-permute-start(bf16[21,128,128]{2,1,0:T(8,128)(2,1)S(1)} %collective-permute-done.3.refs_9_.refs_14_), channel_id=1, source_target_pairs={{0,8},{8,0},{16,24},{24,16},{32,40},{40,32},{48,56},{56,48},{64,72... | collective-permute-start | bytes 2064392 | tf_op jit(solution)/shard_map/ppermute | solution.py:89
  37.2 18.6 %collective-permute-start.13 = (bf16[21,128,128]{2,1,0:T(8,128)(2,1)}, bf16[21,128,128]{2,1,0:T(8,128)(2,1)}, u32[]{:S(2)}, u32[]{:S(2)}) collective-permute-start(bf16[21,128,128]{2,1,0:T(8,128)(2,1)} %collective-permute-done.7.refs_13_.refs_18_), channel_id=1, source_target_pairs={{0,16},{8,24},{16,0},{24,8},{32,48},{40,56},{48,32},{56,40},{64,80... | collective-permute-start | bytes 2064392 | tf_op jit(solution)/shard_map/ppermute | solution.py:89
  42.9 24.3 %collective-permute-start.2 = (bf16[21,128,128]{2,1,0:T(8,128)(2,1)}, bf16[21,128,128]{2,1,0:T(8,128)(2,1)}, u32[]{:S(2)}, u32[]{:S(2)}) collective-permute-start(bf16[21,128,128]{2,1,0:T(8,128)(2,1)} %collective-permute-done.1.refs_7_.refs_12_), channel_id=1, source_target_pairs={{0,8},{8,0},{16,24},{24,16},{32,40},{40,32},{48,56},{56,48},{64,72... | collective-permute-start | bytes 2064392 | tf_op jit(solution)/shard_map/ppermute | solution.py:89
  47.6 19.6 %collective-permute-start.8 = (bf16[21,128,128]{2,1,0:T(8,128)(2,1)}, bf16[21,128,128]{2,1,0:T(8,128)(2,1)}, u32[]{:S(2)}, u32[]{:S(2)}) collective-permute-start(bf16[21,128,128]{2,1,0:T(8,128)(2,1)} %collective-permute-done.7.refs_13_.refs_18_), channel_id=1, source_target_pairs={{0,8},{8,0},{16,24},{24,16},{32,40},{40,32},{48,56},{56,48},{64,72... | collective-permute-start | bytes 2064392 | tf_op jit(solution)/shard_map/ppermute | solution.py:89
  48.5 26.6 %collective-permute-start.12 = (bf16[21,128,128]{2,1,0:T(8,128)(2,1)S(1)}, bf16[21,128,128]{2,1,0:T(8,128)(2,1)}, u32[]{:S(2)}, u32[]{:S(2)}) collective-permute-start(bf16[21,128,128]{2,1,0:T(8,128)(2,1)S(1)} %collective-permute-done.11.refs_9_.refs_17_.refs_22_), channel_id=1, source_target_pairs={{0,8},{8,0},{16,24},{24,16},{32,40},{40,32},{48,56},{56,48},{64,72... | collective-permute-start | bytes 2064392 | tf_op jit(solution)/shard_map/ppermute | solution.py:89
  49.9 25.3 %collective-permute-start.10 = (bf16[21,128,128]{2,1,0:T(8,128)(2,1)}, bf16[21,128,128]{2,1,0:T(8,128)(2,1)}, u32[]{:S(2)}, u32[]{:S(2)}) collective-permute-start(bf16[21,128,128]{2,1,0:T(8,128)(2,1)} %collective-permute-done.9.refs_7_.refs_15_.refs_20_), channel_id=1, source_target_pairs={{0,8},{8,0},{16,24},{24,16},{32,40},{40,32},{48,56},{56,48},{64,72... | collective-permute-start | bytes 2064392 | tf_op jit(solution)/shard_map/ppermute | solution.py:89
  55.8 19.3 %collective-permute-start.14 = (bf16[21,128,128]{2,1,0:T(8,128)(2,1)}, bf16[21,128,128]{2,1,0:T(8,128)(2,1)}, u32[]{:S(2)}, u32[]{:S(2)}) collective-permute-start(bf16[21,128,128]{2,1,0:T(8,128)(2,1)} %collective-permute-done.13.refs_11_.refs_19_.refs_24_), channel_id=1, source_target_pairs={{0,8},{8,0},{16,24},{24,16},{32,40},{40,32},{48,56},{56,48},{64,72... | collective-permute-start | bytes 2064392 | tf_op jit(solution)/shard_map/ppermute | solution.py:89
  86.6 8.5 %collective-permute-start.18 = (bf16[4,21,128,128]{3,2,1,0:T(8,128)(2,1)S(1)}, bf16[4,21,128,128]{3,2,1,0:T(8,128)(2,1)S(1)}, u32[]{:S(2)}, u32[]{:S(2)}) collective-permute-start(bf16[4,21,128,128]{3,2,1,0:T(8,128)(2,1)S(1)} %get-tuple-element.49), channel_id=1, source_target_pairs={{0,8},{8,0},{16,24},{24,16},{32,40},{40,32},{48,56},{56,48},{64,72... | collective-permute-start | bytes 8257544 | tf_op jit(solution)/shard_map/ppermute | solution.py:89
  95.1 42.2 %collective-permute-start.17 = (bf16[4,21,128,128]{3,2,1,0:T(8,128)(2,1)}, bf16[4,21,128,128]{3,2,1,0:T(8,128)(2,1)}, u32[]{:S(2)}, u32[]{:S(2)}) collective-permute-start(bf16[4,21,128,128]{3,2,1,0:T(8,128)(2,1)} %get-tuple-element.47), channel_id=1, source_target_pairs={{0,8},{8,0},{16,24},{24,16},{32,40},{40,32},{48,56},{56,48},{64,72... | collective-permute-start | bytes 8257544 | tf_op jit(solution)/shard_map/ppermute | solution.py:89
  96.9 57.7 %collective-permute-start.24 = (bf16[2,21,128,128]{3,2,1,0:T(8,128)(2,1)}, bf16[2,21,128,128]{3,2,1,0:T(8,128)(2,1)}, u32[]{:S(2)}, u32[]{:S(2)}) collective-permute-start(bf16[2,21,128,128]{3,2,1,0:T(8,128)(2,1)} %add_convert_fusion), channel_id=1, source_target_pairs={{0,96},{8,40},{16,112},{24,56},{32,0},{40,72},{48,16},{56,88},{64,... | collective-permute-start | bytes 4128776 | tf_op jit(solution)/shard_map/ppermute | solution.py:89
  102.2 36.6 %collective-permute-start.19 = (bf16[21,128,128]{2,1,0:T(8,128)(2,1)}, bf16[21,128,128]{2,1,0:T(8,128)(2,1)}, u32[]{:S(2)}, u32[]{:S(2)}) collective-permute-start(bf16[21,128,128]{2,1,0:T(8,128)(2,1)} %get-tuple-element.73), channel_id=1, source_target_pairs={{0,16},{8,24},{16,0},{24,8},{32,48},{40,56},{48,32},{56,40},{64,80... | collective-permute-start | bytes 2064392 | tf_op jit(solution)/shard_map/ppermute | solution.py:89
  115.1 13.2 %copy-start.25 = (bf16[14,192,128]{2,1,0:T(8,128)(2,1)S(1)}, bf16[14,192,128]{2,1,0:T(8,128)(2,1)}, u32[]{:S(2)}) copy-start(bf16[14,192,128]{2,1,0:T(8,128)(2,1)} %copy-done.24) | copy-start | bytes 2064388
  128.1 14.9 %collective-permute-start.31 = (f32[40,128]{1,0:T(8,128)S(1)}, f32[40,128]{1,0:T(8,128)S(1)}, u32[]{:S(2)}, u32[]{:S(2)}) collective-permute-start(f32[40,128]{1,0:T(8,128)S(1)} %get-tuple-element.65), channel_id=1, source_target_pairs={{0,8},{8,0},{16,24},{24,16},{32,40},{40,32},{48,56},{56,48},{64,72... | collective-permute-start | bytes 61448 | tf_op jit(solution)/shard_map/ppermute | solution.py:89
  128.2 23.5 %collective-permute-start.25 = (bf16[21,128,128]{2,1,0:T(8,128)(2,1)}, bf16[21,128,128]{2,1,0:T(8,128)(2,1)}, u32[]{:S(2)}, u32[]{:S(2)}) collective-permute-start(bf16[21,128,128]{2,1,0:T(8,128)(2,1)} %get-tuple-element.72), channel_id=1, source_target_pairs={{0,32},{8,104},{16,48},{24,120},{32,64},{40,8},{48,80},{56,24},{64... | collective-permute-start | bytes 2064392 | tf_op jit(solution)/shard_map/ppermute | solution.py:89
  137.2 12.8 %collective-permute-start.15 = (bf16[2,192,512]{2,1,0:T(8,128)(2,1)}, bf16[2,192,512]{2,1,0:T(8,128)(2,1)S(1)}, u32[]{:S(2)}, u32[]{:S(2)}) collective-permute-start(bf16[2,192,512]{2,1,0:T(8,128)(2,1)} %get-tuple-element.44), channel_id=1, source_target_pairs={{0,2},{1,3},{2,4},{3,5},{4,6},{5,7},{6,0},{7,1},{8,14},{9,15},{10,... | collective-permute-start | bytes 1179656 | tf_op jit(solution)/shard_map/ppermute | solution.py:93
  138.8 11.2 %copy-start.38 = (bf16[2,208,512]{2,1,0:T(8,128)(2,1)S(1)}, bf16[2,208,512]{2,1,0:T(8,128)(2,1)}, u32[]{:S(2)}) copy-start(bf16[2,208,512]{2,1,0:T(8,128)(2,1)} %copy-done.37) | copy-start | bytes 1277956
  141.7 10.1 %copy-start.36 = (bf16[2,208,512]{2,1,0:T(8,128)(2,1)S(1)}, bf16[2,208,512]{2,1,0:T(8,128)(2,1)}, u32[]{:S(2)}) copy-start(bf16[2,208,512]{2,1,0:T(8,128)(2,1)} %copy-done.35) | copy-start | bytes 1277956
  141.7 15.1 %collective-permute-start.20 = (bf16[21,128,128]{2,1,0:T(8,128)(2,1)}, bf16[21,128,128]{2,1,0:T(8,128)(2,1)}, u32[]{:S(2)}, u32[]{:S(2)}) collective-permute-start(bf16[21,128,128]{2,1,0:T(8,128)(2,1)} %fusion.1), channel_id=1, source_target_pairs={{0,32},{8,104},{16,48},{24,120},{32,64},{40,8},{48,80},{56,24},{64... | collective-permute-start | bytes 2064392 | tf_op jit(solution)/shard_map/ppermute | solution.py:89
  143.0 5.5 %collective-permute-start.32 = (f32[40,128]{1,0:T(8,128)S(1)}, f32[40,128]{1,0:T(8,128)S(1)}, u32[]{:S(2)}, u32[]{:S(2)}) collective-permute-start(f32[40,128]{1,0:T(8,128)S(1)} %add.260), channel_id=1, source_target_pairs={{0,16},{8,24},{16,0},{24,8},{32,48},{40,56},{48,32},{56,40},{64,80... | collective-permute-start | bytes 61448 | tf_op jit(solution)/shard_map/ppermute | solution.py:89
  148.5 26.0 %collective-permute-start.21 = (bf16[2,192,512]{2,1,0:T(8,128)(2,1)}, bf16[2,192,512]{2,1,0:T(8,128)(2,1)S(1)}, u32[]{:S(2)}, u32[]{:S(2)}) collective-permute-start(bf16[2,192,512]{2,1,0:T(8,128)(2,1)} %copy-done.39), channel_id=1, source_target_pairs={{0,6},{1,7},{2,0},{3,1},{4,2},{5,3},{6,4},{7,5},{8,10},{9,11},{10,... | collective-permute-start | bytes 1179656 | tf_op jit(solution)/shard_map/ppermute | solution.py:93
  150.1 23.5 %collective-permute-start.27 = (bf16[2,208,512]{2,1,0:T(8,128)(2,1)S(1)}, bf16[2,208,512]{2,1,0:T(8,128)(2,1)S(1)}, u32[]{:S(2)}, u32[]{:S(2)}) collective-permute-start(bf16[2,208,512]{2,1,0:T(8,128)(2,1)S(1)} %copy-done.38), channel_id=1, source_target_pairs={{0,2},{1,3},{2,4},{3,5},{4,6},{5,7},{6,0},{7,1},{8,14},{9,15},{10,... | collective-permute-start | bytes 1277960 | tf_op jit(solution)/shard_map/ppermute | solution.py:93
  151.8 46.8 %collective-permute-start.29 = (bf16[2,208,512]{2,1,0:T(8,128)(2,1)S(1)}, bf16[2,208,512]{2,1,0:T(8,128)(2,1)S(1)}, u32[]{:S(2)}, u32[]{:S(2)}) collective-permute-start(bf16[2,208,512]{2,1,0:T(8,128)(2,1)S(1)} %copy-done.36), channel_id=1, source_target_pairs={{0,6},{1,7},{2,0},{3,1},{4,2},{5,3},{6,4},{7,5},{8,10},{9,11},{10,... | collective-permute-start | bytes 1277960 | tf_op jit(solution)/shard_map/ppermute | solution.py:93
  154.6 15.6 %collective-permute-start.16 = (bf16[2,192,512]{2,1,0:T(8,128)(2,1)S(1)}, bf16[2,192,512]{2,1,0:T(8,128)(2,1)S(1)}, u32[]{:S(2)}, u32[]{:S(2)}) collective-permute-start(bf16[2,192,512]{2,1,0:T(8,128)(2,1)S(1)} %add_convert_fusion.4), channel_id=1, source_target_pairs={{0,2},{1,3},{2,4},{3,5},{4,6},{5,7},{6,0},{7,1},{8,14},{9,15},{10,... | collective-permute-start | bytes 1179656 | tf_op jit(solution)/shard_map/ppermute | solution.py:93
  156.8 18.1 %copy-start.30 = (bf16[2,192,512]{2,1,0:T(8,128)(2,1)S(1)}, bf16[2,192,512]{2,1,0:T(8,128)(2,1)}, u32[]{:S(2)}) copy-start(bf16[2,192,512]{2,1,0:T(8,128)(2,1)} %copy-done.29) | copy-start | bytes 1179652
  156.8 13.9 %collective-permute-start.33 = (f32[40,128]{1,0:T(8,128)S(1)}, f32[40,128]{1,0:T(8,128)S(1)}, u32[]{:S(2)}, u32[]{:S(2)}) collective-permute-start(f32[40,128]{1,0:T(8,128)S(1)} %add.261), channel_id=1, source_target_pairs={{0,1},{1,0},{2,3},{3,2},{4,5},{5,4},{6,7},{7,6},{8,9},{9,8},{10,11... | collective-permute-start | bytes 61448 | tf_op jit(solution)/shard_map/ppermute | solution.py:93
  170.2 29.9 %collective-permute-start.23 = (bf16[21,128,128]{2,1,0:T(8,128)(2,1)S(1)}, bf16[21,128,128]{2,1,0:T(8,128)(2,1)S(1)}, u32[]{:S(2)}, u32[]{:S(2)}) collective-permute-start(bf16[21,128,128]{2,1,0:T(8,128)(2,1)S(1)} %fusion.2), channel_id=1, source_target_pairs={{0,32},{8,104},{16,48},{24,120},{32,64},{40,8},{48,80},{56,24},{64... | collective-permute-start | bytes 2064392 | tf_op jit(solution)/shard_map/ppermute | solution.py:89
  170.7 12.4 %collective-permute-start.36 = (f32[40,128]{1,0:T(8,128)S(1)}, f32[40,128]{1,0:T(8,128)S(1)}, u32[]{:S(2)}, u32[]{:S(2)}) collective-permute-start(f32[40,128]{1,0:T(8,128)S(1)} %add.262), channel_id=1, source_target_pairs={{0,96},{8,104},{16,112},{24,120},{32,64},{40,72},{48,80},{56,88},{... | collective-permute-start | bytes 61448 | tf_op jit(solution)/shard_map/ppermute | solution.py:89
  173.5 9.5 %collective-permute-start.35 = (f32[40,128]{1,0:T(8,128)S(1)}, f32[40,128]{1,0:T(8,128)S(1)}, u32[]{:S(2)}, u32[]{:S(2)}) collective-permute-start(f32[40,128]{1,0:T(8,128)S(1)} %add.262), channel_id=1, source_target_pairs={{0,64},{8,72},{16,80},{24,88},{32,96},{40,104},{48,112},{56,120},{... | collective-permute-start | bytes 61448 | tf_op jit(solution)/shard_map/ppermute | solution.py:89
  174.5 8.5 %collective-permute-start.34 = (f32[40,128]{1,0:T(8,128)S(1)}, f32[40,128]{1,0:T(8,128)S(1)}, u32[]{:S(2)}, u32[]{:S(2)}) collective-permute-start(f32[40,128]{1,0:T(8,128)S(1)} %add.262), channel_id=1, source_target_pairs={{0,32},{8,40},{16,48},{24,56},{32,0},{40,8},{48,16},{56,24},{64,96... | collective-permute-start | bytes 61448 | tf_op jit(solution)/shard_map/ppermute | solution.py:89
  175.0 23.6 %copy-start.27 = (bf16[2,208,512]{2,1,0:T(8,128)(2,1)S(1)}, bf16[2,208,512]{2,1,0:T(8,128)(2,1)}, u32[]{:S(2)}) copy-start(bf16[2,208,512]{2,1,0:T(8,128)(2,1)} %copy-done.26) | copy-start | bytes 1277956
  183.0 5.1 %collective-permute-start.39 = (f32[40,128]{1,0:T(8,128)S(1)}, f32[40,128]{1,0:T(8,128)S(1)}, u32[]{:S(2)}, u32[]{:S(2)}) collective-permute-start(f32[40,128]{1,0:T(8,128)S(1)} %add_add_fusion.1), channel_id=1, source_target_pairs={{0,6},{1,7},{2,4},{3,5},{4,2},{5,3},{6,0},{7,1},{8,14},{9,15},{10,... | collective-permute-start | bytes 61448 | tf_op jit(solution)/shard_map/ppermute | solution.py:93
  183.1 5.4 %collective-permute-start.38 = (f32[40,128]{1,0:T(8,128)S(1)}, f32[40,128]{1,0:T(8,128)S(1)}, u32[]{:S(2)}, u32[]{:S(2)}) collective-permute-start(f32[40,128]{1,0:T(8,128)S(1)} %add_add_fusion.1), channel_id=1, source_target_pairs={{0,4},{1,5},{2,6},{3,7},{4,0},{5,1},{6,2},{7,3},{8,12},{9,13},{10,... | collective-permute-start | bytes 61448 | tf_op jit(solution)/shard_map/ppermute | solution.py:93
  184.0 5.1 %collective-permute-start.37 = (f32[40,128]{1,0:T(8,128)S(1)}, f32[40,128]{1,0:T(8,128)S(1)}, u32[]{:S(2)}, u32[]{:S(2)}) collective-permute-start(f32[40,128]{1,0:T(8,128)S(1)} %add_add_fusion.1), channel_id=1, source_target_pairs={{0,2},{1,3},{2,0},{3,1},{4,6},{5,7},{6,4},{7,5},{8,10},{9,11},{10,... | collective-permute-start | bytes 61448 | tf_op jit(solution)/shard_map/ppermute | solution.py:93
  188.1 19.2 %collective-permute-start.26 = (bf16[21,128,128]{2,1,0:T(8,128)(2,1)S(1)}, bf16[21,128,128]{2,1,0:T(8,128)(2,1)S(1)}, u32[]{:S(2)}, u32[]{:S(2)}) collective-permute-start(bf16[21,128,128]{2,1,0:T(8,128)(2,1)S(1)} %fusion), channel_id=1, source_target_pairs={{0,16},{8,24},{16,0},{24,8},{32,48},{40,56},{48,32},{56,40},{64,80... | collective-permute-start | bytes 2064392 | tf_op jit(solution)/shard_map/ppermute | solution.py:89
  188.5 21.7 %collective-permute-start.22 = (bf16[192,512]{1,0:T(8,128)(2,1)S(1)}, bf16[192,512]{1,0:T(8,128)(2,1)S(1)}, u32[]{:S(2)}, u32[]{:S(2)}) collective-permute-start(bf16[192,512]{1,0:T(8,128)(2,1)S(1)} %fusion.15), channel_id=1, source_target_pairs={{0,1},{1,0},{2,3},{3,2},{4,5},{5,4},{6,7},{7,6},{8,9},{9,8},{10,11... | collective-permute-start | bytes 589832 | tf_op jit(solution)/shard_map/ppermute | solution.py:93
  189.2 9.3 %collective-permute-start.28 = (bf16[2,208,512]{2,1,0:T(8,128)(2,1)S(1)}, bf16[2,208,512]{2,1,0:T(8,128)(2,1)S(1)}, u32[]{:S(2)}, u32[]{:S(2)}) collective-permute-start(bf16[2,208,512]{2,1,0:T(8,128)(2,1)S(1)} %add_convert_fusion.3), channel_id=1, source_target_pairs={{0,2},{1,3},{2,4},{3,5},{4,6},{5,7},{6,0},{7,1},{8,14},{9,15},{10,... | collective-permute-start | bytes 1277960 | tf_op jit(solution)/shard_map/ppermute | solution.py:93
  198.7 11.4 %collective-permute-start.30 = (bf16[208,512]{1,0:T(8,128)(2,1)S(1)}, bf16[208,512]{1,0:T(8,128)(2,1)S(1)}, u32[]{:S(2)}, u32[]{:S(2)}) collective-permute-start(bf16[208,512]{1,0:T(8,128)(2,1)S(1)} %fusion.14), channel_id=1, source_target_pairs={{0,1},{1,0},{2,3},{3,2},{4,5},{5,4},{6,7},{7,6},{8,9},{9,8},{10,11... | collective-permute-start | bytes 638984 | tf_op jit(solution)/shard_map/ppermute | solution.py:93
  (36 other events, 159.1 us)
